TPU v7x, 32 devices: a whole 2x2x4 slice. The times are simulated.
32 devices in a mesh: tm: 4 (over z), gx: 2 (over x), gy: 4 (over y, core).
Axes of the slice: x: 2, y: 2, z: 4, core: 2. Of those that a mesh axis runs over, the one named last changes fastest.
Arguments:
- state_starts: float32 [4, 64, 64, 512], P('tm', None, 'gx', 'gy'), may hold values from -4 to 4, as said below
- diffusivity: float32 [64], replicated, may hold values from 0.3 to 1.2
- wind: float32 [2, 64], replicated, may hold values from -0.6 to 0.6
Outputs:
- segment_ends: float32 [4, 64, 64, 512], P('tm', None, 'gx', 'gy')
Inputs may be any that keep to these rules, and one draw needn't show every extreme that they name: `state_starts`: states of order one.
All inputs are finite; a program needn't handle non-finite values.
Results may differ from a plain program's by a relative error of at most 0.0001.
Values sent between devices are 32-bit elements; how exact they have to be, the bound alone decides.
A program may use at most 64 MiB of HBM per device.

v0:
```python
import functools

import jax
import jax.numpy as jnp
from jax import lax
from jax.experimental import pallas as pl
from jax.experimental.pallas import tpu as pltpu
from jax.sharding import PartitionSpec as P

SUB = 4
REACH = SUB
RATIO = 4
LANES = 128
EDGE = 8
FRONT = 2 * EDGE
COARSE_REACH = 2

time_step = 0.2
weights_low = (0.375, 0.125, 0.0, 0.0)
weights_mid = (0.625, 0.875, 0.875, 0.625)
weights_high = (0.0, 0.0, 0.125, 0.375)
mean_side, mean_mid = 0.125, 0.75

PLANE = tuple((dx, dy) for dx in (-1, 0, 1) for dy in (-1, 0, 1))
AROUND = tuple(d for d in PLANE if d != (0, 0))


def conjunction(conditions):
    total = True
    for condition in conditions:
        total = condition if total is True else jnp.logical_and(total, condition)
    return total


def kernel(
    sizes, levels, rows, cols,
    x_hbm, diff_hbm, wind_hbm, out_ref,
    x_ref, diff_ref, wind_ref, load_sems, ready,
    first, second, x_send, x_recv, y_send, y_recv, corner_recv,
    old_wide, new_wide, extended, old_image, change,
    sent, fine_mean, line, fine_line, spread_rows, turned,
    fine_out, fine_in, old_out, old_in, chain_out, chain_in, *strip_refs,
):
    n_tm, n_gx, n_gy = sizes
    tm, gx, gy = lax.axis_index("tm"), lax.axis_index("gx"), lax.axis_index("gy")
    packs = LANES // levels
    part = rows // packs
    part_c = part // RATIO
    cols_c = cols // RATIO
    wide = part + 2 * REACH
    wide_c = part_c + 2 * COARSE_REACH
    end = FRONT + cols
    end_c = FRONT + cols_c

    def there(dz, dx, dy):
        tests = []
        for place, move, count in ((tm, dz, n_tm), (gx, dx, n_gx), (gy, dy, n_gy)):
            if move < 0:
                tests.append(place > 0)
            if move > 0:
                tests.append(place < count - 1)
        return conjunction(tests)

    def guarded(condition, action):
        if condition is True:
            action()
        else:
            pl.when(condition)(action)

    def target(dz, dx, dy):
        return (tm + dz, gx + dx, gy + dy)

    loads = [
        pltpu.make_async_copy(source, landing, load_sems.at[k])
        for k, (source, landing) in enumerate(((x_hbm, x_ref), (diff_hbm, diff_ref), (wind_hbm, wind_ref)))
    ]
    for load in loads:
        load.start()

    barrier = pltpu.get_barrier_semaphore()
    partners = [(0, dx, dy) for dx, dy in AROUND] + [(-1, 0, 0), (1, 0, 0)]
    partners.sort(key=lambda move: -sum(map(abs, move)))
    awaited = jnp.int32(0)
    for move in partners:
        def greet(move=move):
            pl.semaphore_signal(barrier, inc=1, device_id=target(*move), device_id_type=pl.DeviceIdType.MESH)
        guarded(there(*move), greet)
        awaited = awaited + there(*move).astype(jnp.int32)

    def send_all(copies, dz, moves):
        for move in moves:
            guarded(there(dz, *move), lambda move=move: copies[move].start())

    def sends_done(copies, dz, moves):
        for move in moves:
            guarded(there(dz, *move), lambda move=move: copies[move].wait_send())

    def all_arrived(copies, dz, moves):
        for dx, dy in moves:
            guarded(there(-dz, -dx, -dy), lambda move=(dx, dy): copies[move].wait_recv())

    def remote(source, landing, out_sem, in_sem, move):
        return pltpu.make_async_remote_copy(
            src_ref=source, dst_ref=landing, send_sem=out_sem, recv_sem=in_sem,
            device_id=target(*move), device_id_type=pl.DeviceIdType.MESH,
        )

    def index_of(move):
        return (move[0] + 1) * 3 + move[1] + 1

    fine_copies = {}
    for move in AROUND:
        dx, dy = move
        k = index_of(move)
        if dy == 0:
            source, landing = (buffer.at[(dx + 1) // 2, pl.ds(0, REACH // 2)] for buffer in (x_send, x_recv))
        elif dx == 0:
            source, landing = y_send.at[(dy + 1) // 2], y_recv.at[(1 - dy) // 2]
        else:
            source = y_send.at[(dy + 1) // 2, pl.ds(0 if dx < 0 else part - REACH, REACH)]
            landing = corner_recv.at[(1 - dx) // 2, (1 - dy) // 2]
        fine_copies[move] = remote(source, landing, fine_out.at[k], fine_in.at[k], (0, dx, dy))
    later_copies = {}
    for dx in (-1, 1):
        k = 9 + (dx + 1) // 2
        source, landing = (buffer.at[(dx + 1) // 2, pl.ds(REACH // 2, REACH // 2)] for buffer in (x_send, x_recv))
        later_copies[dx, 0] = remote(source, landing, fine_out.at[k], fine_in.at[k], (0, dx, 0))

    def coarse_copies(main, wide_in, strips, out_sems, in_sems, dz):
        row_out, row_in, side_out, side_in, corner_out, corner_in = strips
        copies = {}
        for dx, dy in PLANE if dz else AROUND:
            k = index_of((dx, dy))
            towards_x, towards_y = (dx + 1) // 2, (dy + 1) // 2
            if dx == 0 and dy == 0:
                source, landing = main, wide_in.at[pl.ds(COARSE_REACH, part_c), pl.ds(FRONT, cols_c)]
            elif dy == 0:
                source, landing = row_out.at[towards_x], row_in.at[towards_x, pl.ds(FRONT, cols_c)]
            elif dx == 0:
                source, landing = side_out.at[towards_y], side_in.at[towards_y]
            else:
                source, landing = corner_out.at[towards_x, towards_y], corner_in.at[towards_x, towards_y]
            copies[dx, dy] = remote(source, landing, out_sems.at[k], in_sems.at[k], (dz, dx, dy))
        return copies

    old_strips, new_strips = strip_refs[:6], strip_refs[6:]
    old_copies = coarse_copies(None, old_wide, old_strips, old_out, old_in, 0)
    chain_copies = coarse_copies(sent, new_wide, new_strips, chain_out, chain_in, 1)

    lane = lax.broadcasted_iota(jnp.int32, (1, LANES), 1)
    pack = lane // levels

    def packed(row):
        return jnp.concatenate([row] * packs, axis=1)

    def advance(source, row, start, count, consts):
        keep, spread, along_x, along_y = consts
        centre = source[row, pl.ds(start, count), :]
        east = source[row + 1, pl.ds(start, count), :]
        west = source[row - 1, pl.ds(start, count), :]
        north = source[row, pl.ds(start + 1, count), :]
        south = source[row, pl.ds(start - 1, count), :]
        pushed = along_x * (east - west) + along_y * (north - south)
        return centre * (keep - pushed) + spread * ((east + west) + (north + south))

    def native_row(x):
        if x < 0:
            return x_recv[1, x + REACH]
        if x >= rows:
            return x_recv[0, x - rows]
        return x_ref[pl.ds(x, levels, stride=rows), :]

    def bring_in(row):
        stacked = jnp.concatenate([native_row(p * part + row - REACH) for p in range(packs)], axis=0)
        first[row, pl.ds(FRONT, cols), :] = stacked.T

    for load in loads:
        load.wait()
    diffuse = packed(diff_ref[...])
    east_wind = packed(wind_ref[0:1, :])
    north_wind = packed(wind_ref[1:2, :])

    def constants(factor):
        spread = (time_step * factor) * diffuse
        return 1.0 - 4.0 * spread, spread, (0.5 * time_step) * east_wind, (0.5 * time_step) * north_wind

    fine_constants = constants(1.0)
    coarse_constants = constants(0.25)

    for r in range(REACH):
        x_send[0, r] = native_row(r)
        x_send[1, r] = native_row(rows - REACH + r)
    x_moves = tuple(m for m in AROUND if m[1] == 0)
    y_moves = tuple(m for m in AROUND if m[1] != 0)
    low_lanes = lane < levels
    high_lanes = lane >= LANES - levels
    pl.semaphore_wait(barrier, awaited)

    @pl.when(tm > 0)
    def _():
        pl.semaphore_signal(ready, inc=1, device_id=target(-1, 0, 0), device_id_type=pl.DeviceIdType.MESH)

    side_moves = tuple(m for m in AROUND if m[0] == 0)
    corner_moves = tuple(m for m in y_moves if m[0] != 0)
    send_all(fine_copies, 0, x_moves)
    for row in range(REACH, REACH + part):
        bring_in(row)
    for row in range(part):
        y_send[0, row] = first[REACH + row, pl.ds(FRONT, REACH), :]
        y_send[1, row] = first[REACH + row, pl.ds(end - REACH, REACH), :]
    send_all(fine_copies, 0, side_moves + corner_moves)

    def restricted(source, row):
        total = source[REACH + row * RATIO, pl.ds(FRONT, cols), :]
        for r in range(1, RATIO):
            total = total + source[REACH + row * RATIO + r, pl.ds(FRONT, cols), :]
        fine_line[...] = total
        mean = fine_line[pl.ds(0, cols_c, stride=RATIO), :]
        for o in range(1, RATIO):
            mean = mean + fine_line[pl.ds(o, cols_c, stride=RATIO), :]
        return mean * (1.0 / RATIO**2)

    def swapped(value):
        return pltpu.roll(value, levels, 1)

    def pack_strips(row_of, strips):
        row_out, _, side_out, _, corner_out, _ = strips
        row_out[0] = jnp.where(low_lanes, row_of(0, 0, cols_c), swapped(row_of(1, 0, cols_c)))
        row_out[1] = jnp.where(low_lanes, swapped(row_of(part_c - 2, 0, cols_c)), row_of(part_c - 1, 0, cols_c))
        for side, col in ((0, 0), (1, cols_c - COARSE_REACH)):
            for row in range(part_c):
                side_out[side, pl.ds(COARSE_REACH * row, COARSE_REACH), :] = row_of(row, col, COARSE_REACH)
            for towards in range(2):
                corner_out[towards, side, pl.ds(0, COARSE_REACH), :] = row_out[towards, pl.ds(col, COARSE_REACH), :]

    def old_row(row, col, count):
        return old_wide[COARSE_REACH + row, pl.ds(FRONT + col, count), :]

    for row in range(part_c):
        old_wide[COARSE_REACH + row, pl.ds(FRONT, cols_c), :] = restricted(first, row)
    pack_strips(old_row, old_strips)
    send_all(old_copies, 0, AROUND)
    send_all(later_copies, 0, x_moves)

    def inside_x(row, reach, length):
        place = (gx * packs + pack) * length + (row - reach)
        return jnp.logical_and(place >= 0, place < n_gx * packs * length)

    def inside_y(start, count, length):
        place = gy * length + (start - FRONT) + lax.broadcasted_iota(jnp.int32, (count, LANES), 0)
        return jnp.logical_and(place >= 0, place < n_gy * length)

    edges = ((FRONT - EDGE, inside_y(FRONT - EDGE, EDGE, cols)), (end, inside_y(end, EDGE, cols)))
    reaches = ((FRONT - REACH, inside_y(FRONT - REACH, REACH, cols)), (end, inside_y(end, REACH, cols)))
    halo_rows = [*range(REACH), *range(REACH + part, wide)]
    half = cols // 2

    def update(source, dest, row, consts, last):
        for start, count in ((FRONT, half), (FRONT + half, cols - half)):
            dest[row, pl.ds(start, count), :] = advance(source, row, start, count, consts)
        if not last:
            for start, mask in edges:
                value = advance(source, row, start, EDGE, consts)
                dest[row, pl.ds(start, EDGE), :] = jnp.where(mask, value, 0.0)

    buffers = (first, second)

    all_arrived(fine_copies, 0, side_moves)
    for side, (start, mask) in enumerate(reaches):
        for row in range(part):
            first[REACH + row, pl.ds(start, REACH), :] = jnp.where(mask, y_recv[side, row], 0.0)
    for step in range(1, SUB + 1):
        def inner_row(row, step=step):
            update(buffers[(step - 1) % 2], buffers[step % 2], row, fine_constants, step == SUB)

        pl.loop(REACH + step, REACH + part - step, unroll=2)(inner_row)

    count_c = cols_c + 2 * EDGE
    begin_c = FRONT - EDGE
    mask_y = inside_y(begin_c, count_c, cols_c)

    def extend(buffer, strips):
        _, row_in, _, side_in, _, corner_in = strips
        for side, col in ((0, end_c), (1, FRONT - COARSE_REACH)):
            for row in range(part_c):
                buffer[COARSE_REACH + row, pl.ds(col, COARSE_REACH), :] = side_in[
                    side, pl.ds(COARSE_REACH * row, COARSE_REACH), :
                ]
            for towards in range(2):
                row_in[towards, pl.ds(col, COARSE_REACH), :] = corner_in[towards, side, pl.ds(0, COARSE_REACH), :]

        def own(row):
            return buffer[COARSE_REACH + row, pl.ds(begin_c, count_c), :]

        above, below = (row_in[towards, pl.ds(begin_c, count_c), :] for towards in (0, 1))
        values = [
            jnp.where(low_lanes, below, swapped(own(part_c - 2))),
            swapped(jnp.where(high_lanes, below, own(part_c - 1))),
            *[own(row) for row in range(part_c)],
            swapped(jnp.where(low_lanes, above, own(0))),
            jnp.where(high_lanes, above, swapped(own(1))),
        ]
        for row, value in enumerate(values):
            mask = mask_y
            if not COARSE_REACH <= row < COARSE_REACH + part_c:
                mask = jnp.logical_and(mask_y, inside_x(row, COARSE_REACH, part_c))
            extended[row, pl.ds(begin_c, count_c), :] = jnp.where(mask, value, 0.0)

    all_arrived(old_copies, 0, AROUND)
    sends_done(old_copies, 0, AROUND)
    extend(old_wide, old_strips)
    for row in range(1, wide_c - 1):
        old_image[row - 1] = advance(extended, row, begin_c, count_c, coarse_constants)


    def compute_change():
        for row in range(1, wide_c - 1):
            moved = advance(extended, row, begin_c, count_c, coarse_constants) - old_image[row - 1]
            mask = jnp.logical_and(mask_y, inside_x(row, COARSE_REACH, part_c))
            change[row - 1, pl.ds(begin_c, count_c), :] = jnp.where(mask, moved, 0.0)

    def change_row(row):
        return change[row, pl.ds(begin_c, count_c), :]

    def smoothed(row):
        line[pl.ds(begin_c, count_c), :] = (
            mean_side * (change_row(row) + change_row(row + 2)) + mean_mid * change_row(row + 1)
        )
        sides = line[pl.ds(FRONT - 1, cols_c), :] + line[pl.ds(FRONT + 1, cols_c), :]
        return mean_side * sides + mean_mid * line[pl.ds(FRONT, cols_c), :]

    @pl.when(tm == 0)
    def _():
        compute_change()
        for row in range(part_c):
            sent[row] = smoothed(row)

    all_arrived(fine_copies, 0, x_moves)
    all_arrived(later_copies, 0, x_moves)
    for row in halo_rows:
        bring_in(row)
        inner = first[row, pl.ds(FRONT, cols), :]
        first[row, pl.ds(FRONT, cols), :] = jnp.where(inside_x(row, REACH, part), inner, 0.0)
    all_arrived(fine_copies, 0, corner_moves)
    for side, (start, mask_side) in enumerate(reaches):
        for row in halo_rows:
            if row < REACH:
                here = jnp.where(high_lanes, corner_recv[0, side, row], y_recv[side, row + part - REACH])
                here = pltpu.roll(here, levels, 1)
            else:
                here = jnp.where(low_lanes, corner_recv[1, side, row - part - REACH], y_recv[side, row - part - REACH])
                here = pltpu.roll(here, LANES - levels, 1)
            mask = jnp.logical_and(mask_side, inside_x(row, REACH, part))
            first[row, pl.ds(start, REACH), :] = jnp.where(mask, here, 0.0)
    for step in range(1, SUB + 1):
        def outer_row(row, step=step):
            for shifted in (row, row + part + REACH - 2 * step):
                mask_x = inside_x(shifted, REACH, part)
                consts = tuple(jnp.where(mask_x, c, 0.0) for c in fine_constants)
                update(buffers[(step - 1) % 2], buffers[step % 2], shifted, consts, step == SUB)

        pl.loop(step, REACH + step)(outer_row)
    fine = buffers[SUB % 2]

    for row in range(part_c):
        fine_mean[row] = restricted(fine, row)

    def write_fine():
        for row in range(part):
            turned[row] = fine[REACH + row, pl.ds(FRONT, cols), :].T

    def pass_on():
        pl.semaphore_wait(ready, 1)
        pack_strips(lambda row, col, count: sent[row, pl.ds(col, count), :], new_strips)
        send_all(chain_copies, 1, AROUND)
        send_all(chain_copies, 1, ((0, 0),))

    @pl.when(jnp.logical_and(tm == 0, tm < n_tm - 1))
    def _():
        for row in range(part_c):
            sent[row] = fine_mean[row] + sent[row]
        pass_on()

    write_fine()

    @pl.when(tm > 0)
    def _():
        all_arrived(chain_copies, 1, PLANE)
        extend(new_wide, new_strips)
        compute_change()

    @pl.when(jnp.logical_and(tm > 0, tm < n_tm - 1))
    def _():
        for row in range(part_c):
            sent[row] = fine_mean[row] + smoothed(row)
        pass_on()

    coarse_col = lax.broadcasted_iota(jnp.int32, (count_c, cols), 0) - EDGE
    fine_col = lax.broadcasted_iota(jnp.int32, (count_c, cols), 1)
    offset_of = fine_col & (RATIO - 1)
    apart = coarse_col - (fine_col >> (RATIO.bit_length() - 1))
    spreading = jnp.zeros((count_c, cols), jnp.float32)
    for o in range(RATIO):
        for distance, weights in ((-1, weights_low), (0, weights_mid), (1, weights_high)):
            chosen = jnp.logical_and(offset_of == o, apart == distance)
            spreading = jnp.where(chosen, weights[o], spreading)
    spreading = jnp.concatenate([spreading.astype(jnp.bfloat16)] * 3, axis=0)
    for row in range(part_c + 2):
        rest, pieces = change_row(row), []
        for _ in range(3):
            piece = rest.astype(jnp.bfloat16).astype(jnp.float32)
            pieces.append(piece)
            rest = rest - piece
        split = jnp.concatenate(pieces, axis=0).T.astype(jnp.bfloat16)
        spread_rows[row] = jnp.dot(split, spreading, preferred_element_type=jnp.float32)

    for row in range(part):
        at, o = row // RATIO, row % RATIO
        total = turned[row] + weights_mid[o] * spread_rows[at + 1]
        if weights_low[o]:
            total = total + weights_low[o] * spread_rows[at]
        if weights_high[o]:
            total = total + weights_high[o] * spread_rows[at + 2]
        for p in range(packs):
            out_ref[pl.ds(p * part + row, levels, stride=rows), :] = total[p * levels : (p + 1) * levels]

    sends_done(fine_copies, 0, AROUND)
    sends_done(later_copies, 0, x_moves)
    pl.when(tm < n_tm - 1)(lambda: sends_done(chain_copies, 1, PLANE))


def shards(sizes, state_starts, diffusivity, wind):
    _, levels, rows, cols = state_starts.shape
    packs = LANES // levels
    if packs != 2 or levels * packs != LANES:
        raise ValueError(levels)
    part = rows // packs
    part_c = part // RATIO
    cols_c = cols // RATIO
    wide, wide_c = part + 2 * REACH, part_c + 2 * COARSE_REACH
    vmem = functools.partial(pltpu.VMEM, dtype=jnp.float32)
    scratch = [
        vmem((levels * rows, cols)),
        vmem((1, levels)),
        vmem((2, levels)),
        pltpu.SemaphoreType.DMA((3,)),
        pltpu.SemaphoreType.REGULAR,
        vmem((wide, cols + 2 * FRONT, LANES)),
        vmem((wide, cols + 2 * FRONT, LANES)),
        vmem((2, REACH, levels, cols)),
        vmem((2, REACH, levels, cols)),
        vmem((2, part, REACH, LANES)),
        vmem((2, part, REACH, LANES)),
        vmem((2, 2, REACH, REACH, LANES)),
        vmem((wide_c, cols_c + 2 * FRONT, LANES)),
        vmem((wide_c, cols_c + 2 * FRONT, LANES)),
        vmem((wide_c, cols_c + 2 * FRONT, LANES)),
        vmem((wide_c - 2, cols_c + 2 * EDGE, LANES)),
        vmem((wide_c - 2, cols_c + 2 * FRONT, LANES)),
        vmem((part_c, cols_c, LANES)),
        vmem((part_c, cols_c, LANES)),
        vmem((cols_c + 2 * FRONT, LANES)),
        vmem((cols, LANES)),
        vmem((part_c + 2, LANES, cols)),
        vmem((part, LANES, cols)),
    ] + [pltpu.SemaphoreType.DMA((11,))] * 2 + [pltpu.SemaphoreType.DMA((9,))] * 4
    scratch += [
        vmem((2, cols_c, LANES)),
        vmem((2, cols_c + 2 * FRONT, LANES)),
        vmem((2, COARSE_REACH * part_c, LANES)),
        vmem((2, COARSE_REACH * part_c, LANES)),
        vmem((2, 2, EDGE, LANES)),
        vmem((2, 2, EDGE, LANES)),
    ] * 2
    in_vmem = pl.BlockSpec(memory_space=pltpu.VMEM)
    ending = pl.pallas_call(
        functools.partial(kernel, sizes, levels, rows, cols),
        out_shape=pltpu.VMEM((levels * rows, cols), jnp.float32),
        in_specs=[pl.BlockSpec(memory_space=pl.ANY)] * 3,
        out_specs=in_vmem,
        scratch_shapes=scratch,
        compiler_params=pltpu.CompilerParams(collective_id=0, has_side_effects=True),
        name="parareal",
    )(state_starts.reshape(levels * rows, cols), diffusivity.reshape(1, levels), wind)
    return ending.reshape(1, levels, rows, cols)


def solution(mesh):
    sizes = tuple(mesh.shape[axis] for axis in ("tm", "gx", "gy"))
    placed = (P("tm", None, "gx", "gy"), P(), P())
    return jax.shard_map(
        functools.partial(shards, sizes),
        mesh=mesh, in_specs=placed, out_specs=P("tm", None, "gx", "gy"), check_vma=False,
    )
```

profile of v0, /device:TPU:24, one launch (start us, length us, event | category | flops | bytes accessed | tf_op | source)
XLA Modules:
  0.0 22.1 jit_solution(16082883794971019372)
XLA Ops:
  0.0 21.1 %parareal.1 = f32[2048,128]{1,0:T(8,128)S(1)} custom-call(f32[2048,128]{1,0:T(8,128)} %bitcast.4, f32[1,64]{1,0:T(1,128)} %bitcast.5, f32[2,64]{1,0:T(2,128)} %wind_hbm.1), custom_call_target="tpu_custom_call" | custom-call | tf_op jit(solution)/shard_map/parareal/pallas_call | solution.py:476
  21.1 1.0 %copy.5 = f32[1,64,32,128]{3,2,1,0:T(8,128)} copy(f32[1,64,32,128]{3,2,1,0:T(8,128)S(1)} %bitcast.3) | data formatting | bytes 2097152
where the time goes:
time: 22.3 us; the launch traced here: 22.1 us
  Pallas kernels  21.1 us (95%)
  local copies, waits for them, and re-layouts  0.97 us (4%)
    pallas_call x1, Pallas kernels, shards(): pl.pallas_call(functools.partial(kernel, sizes, levels, rows, cols), out_...  21.1 us
    unnamed x1, local copies, waits for them, and re-layouts  0.97 us

commit v1 on v0

--- a/solution.py
+++ b/solution.py
@@ -14,6 +14,7 @@
 EDGE = 8
 FRONT = 2 * EDGE
 COARSE_REACH = 2
+BLOCKS = 4
 
 time_step = 0.2
 weights_low = (0.375, 0.125, 0.0, 0.0)
@@ -34,11 +35,11 @@
 
 def kernel(
     sizes, levels, rows, cols,
-    x_hbm, diff_hbm, wind_hbm, out_ref,
+    x_hbm, diff_hbm, wind_hbm, turned, spread_rows,
     x_ref, diff_ref, wind_ref, load_sems, ready,
     first, second, x_send, x_recv, y_send, y_recv, corner_recv,
     old_wide, new_wide, extended, old_image, change,
-    sent, fine_mean, line, fine_line, spread_rows, turned,
+    sent, fine_mean, line, fine_line,
     fine_out, fine_in, old_out, old_in, chain_out, chain_in, *strip_refs,
 ):
     n_tm, n_gx, n_gy = sizes
@@ -414,19 +415,33 @@
         split = jnp.concatenate(pieces, axis=0).T.astype(jnp.bfloat16)
         spread_rows[row] = jnp.dot(split, spreading, preferred_element_type=jnp.float32)
 
-    for row in range(part):
-        at, o = row // RATIO, row % RATIO
-        total = turned[row] + weights_mid[o] * spread_rows[at + 1]
-        if weights_low[o]:
-            total = total + weights_low[o] * spread_rows[at]
-        if weights_high[o]:
-            total = total + weights_high[o] * spread_rows[at + 2]
-        for p in range(packs):
-            out_ref[pl.ds(p * part + row, levels, stride=rows), :] = total[p * levels : (p + 1) * levels]
-
     sends_done(fine_copies, 0, AROUND)
     sends_done(later_copies, 0, x_moves)
     pl.when(tm < n_tm - 1)(lambda: sends_done(chain_copies, 1, PLANE))
+
+
+def closing(levels, rows, turned, spread_rows, out_hbm, filled, sems):
+    packs = LANES // levels
+    part = rows // packs
+    blocks = filled.shape[0]
+    block = levels // blocks
+    copies = []
+    for k in range(blocks):
+        for row in range(part):
+            at, o = row // RATIO, row % RATIO
+            for p in range(packs):
+                here = pl.ds(p * levels + k * block, block)
+                total = turned[row, here, :] + weights_mid[o] * spread_rows[at + 1, here, :]
+                if weights_low[o]:
+                    total = total + weights_low[o] * spread_rows[at, here, :]
+                if weights_high[o]:
+                    total = total + weights_high[o] * spread_rows[at + 2, here, :]
+                filled[k, pl.ds(p * part + row, block, stride=rows), :] = total
+        copy = pltpu.make_async_copy(filled.at[k], out_hbm.at[pl.ds(k * block * rows, block * rows)], sems.at[k])
+        copy.start()
+        copies.append(copy)
+    for copy in copies:
+        copy.wait()
 
 
 def shards(sizes, state_starts, diffusivity, wind):
@@ -461,8 +476,6 @@
         vmem((part_c, cols_c, LANES)),
         vmem((cols_c + 2 * FRONT, LANES)),
         vmem((cols, LANES)),
-        vmem((part_c + 2, LANES, cols)),
-        vmem((part, LANES, cols)),
     ] + [pltpu.SemaphoreType.DMA((11,))] * 2 + [pltpu.SemaphoreType.DMA((9,))] * 4
     scratch += [
         vmem((2, cols_c, LANES)),
@@ -473,15 +486,26 @@
         vmem((2, 2, EDGE, LANES)),
     ] * 2
     in_vmem = pl.BlockSpec(memory_space=pltpu.VMEM)
-    ending = pl.pallas_call(
+    turned, spread_rows = pl.pallas_call(
         functools.partial(kernel, sizes, levels, rows, cols),
-        out_shape=pltpu.VMEM((levels * rows, cols), jnp.float32),
+        out_shape=(vmem((part, LANES, cols)), vmem((part_c + 2, LANES, cols))),
         in_specs=[pl.BlockSpec(memory_space=pl.ANY)] * 3,
-        out_specs=in_vmem,
+        out_specs=(in_vmem, in_vmem),
         scratch_shapes=scratch,
         compiler_params=pltpu.CompilerParams(collective_id=0, has_side_effects=True),
         name="parareal",
     )(state_starts.reshape(levels * rows, cols), diffusivity.reshape(1, levels), wind)
+    ending = pl.pallas_call(
+        functools.partial(closing, levels, rows),
+        out_shape=jax.ShapeDtypeStruct((levels * rows, cols), jnp.float32),
+        in_specs=[in_vmem, in_vmem],
+        out_specs=pl.BlockSpec(memory_space=pl.ANY),
+        scratch_shapes=[
+            vmem((BLOCKS, levels // BLOCKS * rows, cols)),
+            pltpu.SemaphoreType.DMA((BLOCKS,)),
+        ],
+        name="closing",
+    )(*(pltpu.with_memory_space_constraint(array, pltpu.VMEM) for array in (turned, spread_rows)))
     return ending.reshape(1, levels, rows, cols)
 
 

time: 22.3 us -> 22.4 us (level)
  Pallas kernels: 21.1 us -> 22.1 us
  local copies, waits for them, and re-layouts: 0.97 us -> 0 us
    pallas_call x0 -> x1, Pallas kernels: none -> 1.64 us  [shards(): pl.pallas_call(functools.partial(closing, levels, rows), out_shape=jax.Sh...]
    unnamed x1 -> x0, local copies, waits for them, and re-layouts: 0.97 us -> none
    pallas_call x1, Pallas kernels: 21.1 us -> 20.5 us  [shards(): pl.pallas_call(functools.partial(kernel, sizes, levels, rows, cols), out_...]
where the time goes in v1:
time: 22.4 us; the launch traced here: 22.1 us
  Pallas kernels  22.1 us (99%)
    pallas_call x1, Pallas kernels, shards(): pl.pallas_call(functools.partial(kernel, sizes, levels, rows, cols), out_...  20.5 us
    pallas_call x1, Pallas kernels, shards(): pl.pallas_call(functools.partial(closing, levels, rows), out_shape=jax.Sh...  1.64 us

profile of v1, /device:TPU:24, one launch (start us, length us, event | category | flops | bytes accessed | tf_op | source)
XLA Modules:
  0.0 22.1 jit_solution(17334712962028653483)
XLA Ops:
  0.0 20.5 %parareal.1 = (f32[16,128,128]{2,1,0:T(8,128)S(1)}, f32[6,128,128]{2,1,0:T(8,128)S(1)}) custom-call(f32[2048,128]{1,0:T(8,128)} %bitcast.3, f32[1,64]{1,0:T(1,128)} %bitcast.4, f32[2,64]{1,0:T(2,128)} %wind_hbm.1), custom_call_target="tpu_custom_call" | custom-call | tf_op jit(solution)/shard_map/parareal/pallas_call | solution.py:489
  20.5 1.6 %closing.1 = f32[2048,128]{1,0:T(8,128)} custom-call(f32[16,128,128]{2,1,0:T(8,128)S(1)} %get-tuple-element.7.turned, f32[6,128,128]{2,1,0:T(8,128)S(1)} %get-tuple-element.8.spread_rows), custom_call_target="tpu_custom_call" | custom-call | tf_op jit(solution)/shard_map/closing/pallas_call | solution.py:498

commit v2 on v0

--- a/solution.py
+++ b/solution.py
@@ -34,12 +34,12 @@
 
 def kernel(
     sizes, levels, rows, cols,
-    x_hbm, diff_hbm, wind_hbm, out_ref,
-    x_ref, diff_ref, wind_ref, load_sems, ready,
-    first, second, x_send, x_recv, y_send, y_recv, corner_recv,
-    old_wide, new_wide, extended, old_image, change,
-    sent, fine_mean, line, fine_line, spread_rows, turned,
-    fine_out, fine_in, old_out, old_in, chain_out, chain_in, *strip_refs,
+    x_hbm, diff_hbm, wind_hbm, turned, change,
+    x_ref, diff_ref, wind_ref, load_sems, small_sems, ready,
+    first, second, x_recv, y_send, y_recv, corner_recv,
+    old_wide, new_wide, extended, old_image,
+    sent, fine_mean, line, fine_line,
+    x_out, x_in, fine_out, fine_in, old_out, old_in, chain_out, chain_in, *strip_refs,
 ):
     n_tm, n_gx, n_gy = sizes
     tm, gx, gy = lax.axis_index("tm"), lax.axis_index("gx"), lax.axis_index("gy")
@@ -70,11 +70,15 @@
     def target(dz, dx, dy):
         return (tm + dz, gx + dx, gy + dy)
 
-    loads = [
-        pltpu.make_async_copy(source, landing, load_sems.at[k])
-        for k, (source, landing) in enumerate(((x_hbm, x_ref), (diff_hbm, diff_ref), (wind_hbm, wind_ref)))
+    small_loads = [
+        pltpu.make_async_copy(source, landing, small_sems.at[k])
+        for k, (source, landing) in enumerate(((diff_hbm, diff_ref), (wind_hbm, wind_ref)))
     ]
-    for load in loads:
+    loads = {x: pltpu.make_async_copy(x_hbm.at[:, x], x_ref.at[x], load_sems.at[x]) for x in range(rows)}
+    by_row = [p * part + row for row in range(part) for p in range(packs)]
+    for x in by_row:
+        loads[x].start()
+    for load in small_loads:
         load.start()
 
     barrier = pltpu.get_barrier_semaphore()
@@ -113,18 +117,22 @@
         dx, dy = move
         k = index_of(move)
         if dy == 0:
-            source, landing = (buffer.at[(dx + 1) // 2, pl.ds(0, REACH // 2)] for buffer in (x_send, x_recv))
-        elif dx == 0:
+            continue
+        if dx == 0:
             source, landing = y_send.at[(dy + 1) // 2], y_recv.at[(1 - dy) // 2]
         else:
             source = y_send.at[(dy + 1) // 2, pl.ds(0 if dx < 0 else part - REACH, REACH)]
             landing = corner_recv.at[(1 - dx) // 2, (1 - dy) // 2]
         fine_copies[move] = remote(source, landing, fine_out.at[k], fine_in.at[k], (0, dx, dy))
-    later_copies = {}
-    for dx in (-1, 1):
-        k = 9 + (dx + 1) // 2
-        source, landing = (buffer.at[(dx + 1) // 2, pl.ds(REACH // 2, REACH // 2)] for buffer in (x_send, x_recv))
-        later_copies[dx, 0] = remote(source, landing, fine_out.at[k], fine_in.at[k], (0, dx, 0))
+    x_copies = []
+    for r in range(REACH):
+        copies = {}
+        for dx in (-1, 1):
+            towards = (dx + 1) // 2
+            k = towards * REACH + r
+            source = x_hbm.at[:, r if dx < 0 else rows - REACH + r]
+            copies[dx, 0] = remote(source, x_recv.at[towards, r], x_out.at[k], x_in.at[k], (0, dx, 0))
+        x_copies.append(copies)
 
     def coarse_copies(main, wide_in, strips, out_sems, in_sems, dz):
         row_out, row_in, side_out, side_in, corner_out, corner_in = strips
@@ -168,28 +176,12 @@
             return x_recv[1, x + REACH]
         if x >= rows:
             return x_recv[0, x - rows]
-        return x_ref[pl.ds(x, levels, stride=rows), :]
+        return x_ref[x]
 
     def bring_in(row):
         stacked = jnp.concatenate([native_row(p * part + row - REACH) for p in range(packs)], axis=0)
         first[row, pl.ds(FRONT, cols), :] = stacked.T
 
-    for load in loads:
-        load.wait()
-    diffuse = packed(diff_ref[...])
-    east_wind = packed(wind_ref[0:1, :])
-    north_wind = packed(wind_ref[1:2, :])
-
-    def constants(factor):
-        spread = (time_step * factor) * diffuse
-        return 1.0 - 4.0 * spread, spread, (0.5 * time_step) * east_wind, (0.5 * time_step) * north_wind
-
-    fine_constants = constants(1.0)
-    coarse_constants = constants(0.25)
-
-    for r in range(REACH):
-        x_send[0, r] = native_row(r)
-        x_send[1, r] = native_row(rows - REACH + r)
     x_moves = tuple(m for m in AROUND if m[1] == 0)
     y_moves = tuple(m for m in AROUND if m[1] != 0)
     low_lanes = lane < levels
@@ -202,8 +194,24 @@
 
     side_moves = tuple(m for m in AROUND if m[0] == 0)
     corner_moves = tuple(m for m in y_moves if m[0] != 0)
-    send_all(fine_copies, 0, x_moves)
+    for copies in x_copies[: REACH // 2]:
+        send_all(copies, 0, x_moves)
+    for load in small_loads:
+        load.wait()
+    diffuse = packed(diff_ref[...])
+    east_wind = packed(wind_ref[0:1, :])
+    north_wind = packed(wind_ref[1:2, :])
+
+    def constants(factor):
+        spread = (time_step * factor) * diffuse
+        return 1.0 - 4.0 * spread, spread, (0.5 * time_step) * east_wind, (0.5 * time_step) * north_wind
+
+    fine_constants = constants(1.0)
+    coarse_constants = constants(0.25)
+
     for row in range(REACH, REACH + part):
+        for p in range(packs):
+            loads[p * part + row - REACH].wait()
         bring_in(row)
     for row in range(part):
         y_send[0, row] = first[REACH + row, pl.ds(FRONT, REACH), :]
@@ -240,7 +248,8 @@
         old_wide[COARSE_REACH + row, pl.ds(FRONT, cols_c), :] = restricted(first, row)
     pack_strips(old_row, old_strips)
     send_all(old_copies, 0, AROUND)
-    send_all(later_copies, 0, x_moves)
+    for copies in x_copies[REACH // 2 :]:
+        send_all(copies, 0, x_moves)
 
     def inside_x(row, reach, length):
         place = (gx * packs + pack) * length + (row - reach)
@@ -335,8 +344,8 @@
         for row in range(part_c):
             sent[row] = smoothed(row)
 
-    all_arrived(fine_copies, 0, x_moves)
-    all_arrived(later_copies, 0, x_moves)
+    for copies in x_copies:
+        all_arrived(copies, 0, x_moves)
     for row in halo_rows:
         bring_in(row)
         inner = first[row, pl.ds(FRONT, cols), :]
@@ -395,6 +404,17 @@
             sent[row] = fine_mean[row] + smoothed(row)
         pass_on()
 
+    sends_done(fine_copies, 0, y_moves)
+    for copies in x_copies:
+        sends_done(copies, 0, x_moves)
+    pl.when(tm < n_tm - 1)(lambda: sends_done(chain_copies, 1, PLANE))
+
+
+def closing(levels, rows, turned, change, out_hbm, filled, spread_rows, sems):
+    packs = LANES // levels
+    part, _, cols = turned.shape
+    part_c = part // RATIO
+    count_c = cols // RATIO + 2 * EDGE
     coarse_col = lax.broadcasted_iota(jnp.int32, (count_c, cols), 0) - EDGE
     fine_col = lax.broadcasted_iota(jnp.int32, (count_c, cols), 1)
     offset_of = fine_col & (RATIO - 1)
@@ -405,28 +425,35 @@
             chosen = jnp.logical_and(offset_of == o, apart == distance)
             spreading = jnp.where(chosen, weights[o], spreading)
     spreading = jnp.concatenate([spreading.astype(jnp.bfloat16)] * 3, axis=0)
-    for row in range(part_c + 2):
-        rest, pieces = change_row(row), []
+    def spread_row(row):
+        rest, pieces = change[row, pl.ds(FRONT - EDGE, count_c), :], []
         for _ in range(3):
             piece = rest.astype(jnp.bfloat16).astype(jnp.float32)
             pieces.append(piece)
             rest = rest - piece
         split = jnp.concatenate(pieces, axis=0).T.astype(jnp.bfloat16)
-        spread_rows[row] = jnp.dot(split, spreading, preferred_element_type=jnp.float32)
-
+        return jnp.dot(split, spreading, preferred_element_type=jnp.float32)
+
+    for row in range(2):
+        spread_rows[row] = spread_row(row)
+    copies = []
     for row in range(part):
         at, o = row // RATIO, row % RATIO
+        if o == 0:
+            spread_rows[at + 2] = spread_row(at + 2)
         total = turned[row] + weights_mid[o] * spread_rows[at + 1]
         if weights_low[o]:
             total = total + weights_low[o] * spread_rows[at]
         if weights_high[o]:
             total = total + weights_high[o] * spread_rows[at + 2]
+        filled[row] = total
         for p in range(packs):
-            out_ref[pl.ds(p * part + row, levels, stride=rows), :] = total[p * levels : (p + 1) * levels]
-
-    sends_done(fine_copies, 0, AROUND)
-    sends_done(later_copies, 0, x_moves)
-    pl.when(tm < n_tm - 1)(lambda: sends_done(chain_copies, 1, PLANE))
+            x = p * part + row
+            copy = pltpu.make_async_copy(filled.at[row, pl.ds(p * levels, levels)], out_hbm.at[:, x], sems.at[x])
+            copy.start()
+            copies.append(copy)
+    for copy in copies:
+        copy.wait()
 
 
 def shards(sizes, state_starts, diffusivity, wind):
@@ -440,14 +467,14 @@
     wide, wide_c = part + 2 * REACH, part_c + 2 * COARSE_REACH
     vmem = functools.partial(pltpu.VMEM, dtype=jnp.float32)
     scratch = [
-        vmem((levels * rows, cols)),
+        vmem((rows, levels, cols)),
         vmem((1, levels)),
         vmem((2, levels)),
-        pltpu.SemaphoreType.DMA((3,)),
+        pltpu.SemaphoreType.DMA((rows,)),
+        pltpu.SemaphoreType.DMA((2,)),
         pltpu.SemaphoreType.REGULAR,
         vmem((wide, cols + 2 * FRONT, LANES)),
         vmem((wide, cols + 2 * FRONT, LANES)),
-        vmem((2, REACH, levels, cols)),
         vmem((2, REACH, levels, cols)),
         vmem((2, part, REACH, LANES)),
         vmem((2, part, REACH, LANES)),
@@ -456,14 +483,11 @@
         vmem((wide_c, cols_c + 2 * FRONT, LANES)),
         vmem((wide_c, cols_c + 2 * FRONT, LANES)),
         vmem((wide_c - 2, cols_c + 2 * EDGE, LANES)),
-        vmem((wide_c - 2, cols_c + 2 * FRONT, LANES)),
         vmem((part_c, cols_c, LANES)),
         vmem((part_c, cols_c, LANES)),
         vmem((cols_c + 2 * FRONT, LANES)),
         vmem((cols, LANES)),
-        vmem((part_c + 2, LANES, cols)),
-        vmem((part, LANES, cols)),
-    ] + [pltpu.SemaphoreType.DMA((11,))] * 2 + [pltpu.SemaphoreType.DMA((9,))] * 4
+    ] + [pltpu.SemaphoreType.DMA((2 * REACH,))] * 2 + [pltpu.SemaphoreType.DMA((9,))] * 6
     scratch += [
         vmem((2, cols_c, LANES)),
         vmem((2, cols_c + 2 * FRONT, LANES)),
@@ -473,15 +497,27 @@
         vmem((2, 2, EDGE, LANES)),
     ] * 2
     in_vmem = pl.BlockSpec(memory_space=pltpu.VMEM)
-    ending = pl.pallas_call(
+    handed = pl.pallas_call(
         functools.partial(kernel, sizes, levels, rows, cols),
-        out_shape=pltpu.VMEM((levels * rows, cols), jnp.float32),
+        out_shape=(vmem((part, LANES, cols)), vmem((part_c + 2, cols_c + 2 * FRONT, LANES))),
         in_specs=[pl.BlockSpec(memory_space=pl.ANY)] * 3,
-        out_specs=in_vmem,
+        out_specs=(in_vmem, in_vmem),
         scratch_shapes=scratch,
         compiler_params=pltpu.CompilerParams(collective_id=0, has_side_effects=True),
         name="parareal",
-    )(state_starts.reshape(levels * rows, cols), diffusivity.reshape(1, levels), wind)
+    )(state_starts.reshape(levels, rows, cols), diffusivity.reshape(1, levels), wind)
+    ending = pl.pallas_call(
+        functools.partial(closing, levels, rows),
+        out_shape=jax.ShapeDtypeStruct((levels, rows, cols), jnp.float32),
+        in_specs=[in_vmem, in_vmem],
+        out_specs=pl.BlockSpec(memory_space=pl.ANY),
+        scratch_shapes=[
+            vmem((part, LANES, cols)),
+            vmem((part_c + 2, LANES, cols)),
+            pltpu.SemaphoreType.DMA((rows,)),
+        ],
+        name="closing",
+    )(*(pltpu.with_memory_space_constraint(array, pltpu.VMEM) for array in handed))
     return ending.reshape(1, levels, rows, cols)
 
 

time: 22.3 us -> 23 us (1.031)
  Pallas kernels: 21.1 us -> 22.9 us
  local copies, waits for them, and re-layouts: 0.97 us -> 0 us
    pallas_call x0 -> x1, Pallas kernels: none -> 1.5 us  [shards(): pl.pallas_call(functools.partial(closing, levels, rows), out_shape=jax.Sh...]
    unnamed x1 -> x0, local copies, waits for them, and re-layouts: 0.97 us -> none
    pallas_call x1, Pallas kernels: 21.1 us -> 21.4 us  [shards(): pl.pallas_call(functools.partial(kernel, sizes, levels, rows, cols), out_...]
where the time goes in v2:
time: 23 us; the launch traced here: 22.9 us
  Pallas kernels  22.9 us (100%)
    pallas_call x1, Pallas kernels, shards(): pl.pallas_call(functools.partial(kernel, sizes, levels, rows, cols), out_...  21.4 us
    pallas_call x1, Pallas kernels, shards(): pl.pallas_call(functools.partial(closing, levels, rows), out_shape=jax.Sh...  1.5 us

profile of v2, /device:TPU:24, one launch (start us, length us, event | category | flops | bytes accessed | tf_op | source)
XLA Modules:
  0.0 22.9 jit_solution(532107103469124822)
XLA Ops:
  0.0 21.4 %parareal.1 = (f32[16,128,128]{2,1,0:T(8,128)S(1)}, f32[6,64,128]{2,1,0:T(8,128)S(1)}) custom-call(f32[64,32,128]{2,1,0:T(8,128)} %bitcast.3, f32[1,64]{1,0:T(1,128)} %bitcast.4, f32[2,64]{1,0:T(2,128)} %wind_hbm.1), custom_call_target="tpu_custom_call" | custom-call | tf_op jit(solution)/shard_map/parareal/pallas_call | solution.py:500
  21.4 1.5 %closing.1 = f32[64,32,128]{2,1,0:T(8,128)} custom-call(f32[16,128,128]{2,1,0:T(8,128)S(1)} %get-tuple-element.7.turned, f32[6,64,128]{2,1,0:T(8,128)S(1)} %get-tuple-element.8.change), custom_call_target="tpu_custom_call" | custom-call | tf_op jit(solution)/shard_map/closing/pallas_call | solution.py:509

commit v3 on v2

--- a/solution.py
+++ b/solution.py
@@ -23,6 +23,10 @@
 
 PLANE = tuple((dx, dy) for dx in (-1, 0, 1) for dy in (-1, 0, 1))
 AROUND = tuple(d for d in PLANE if d != (0, 0))
+x_moves = tuple(d for d in AROUND if d[1] == 0)
+y_moves = tuple(d for d in AROUND if d[1] != 0)
+side_moves = tuple(d for d in y_moves if d[0] == 0)
+corner_moves = tuple(d for d in y_moves if d[0] != 0)
 
 
 def conjunction(conditions):
@@ -35,11 +39,11 @@
 def kernel(
     sizes, levels, rows, cols,
     x_hbm, diff_hbm, wind_hbm, turned, change,
-    x_ref, diff_ref, wind_ref, load_sems, small_sems, ready,
+    x_ref, small_ref, load_sem, small_sem, ready,
     first, second, x_recv, y_send, y_recv, corner_recv,
     old_wide, new_wide, extended, old_image,
     sent, fine_mean, line, fine_line,
-    x_out, x_in, fine_out, fine_in, old_out, old_in, chain_out, chain_in, *strip_refs,
+    out_sem, x_in, fine_in, old_in, chain_in, *strip_refs,
 ):
     n_tm, n_gx, n_gy = sizes
     tm, gx, gy = lax.axis_index("tm"), lax.axis_index("gx"), lax.axis_index("gy")
@@ -70,16 +74,10 @@
     def target(dz, dx, dy):
         return (tm + dz, gx + dx, gy + dy)
 
-    small_loads = [
-        pltpu.make_async_copy(source, landing, small_sems.at[k])
-        for k, (source, landing) in enumerate(((diff_hbm, diff_ref), (wind_hbm, wind_ref)))
-    ]
-    loads = {x: pltpu.make_async_copy(x_hbm.at[:, x], x_ref.at[x], load_sems.at[x]) for x in range(rows)}
-    by_row = [p * part + row for row in range(part) for p in range(packs)]
-    for x in by_row:
-        loads[x].start()
-    for load in small_loads:
-        load.start()
+    for x in range(rows):
+        pltpu.make_async_copy(x_hbm.at[:, x], x_ref.at[x], load_sem).start()
+    for source, landing in ((diff_hbm, small_ref.at[pl.ds(0, 1)]), (wind_hbm, small_ref.at[pl.ds(1, 2)])):
+        pltpu.make_async_copy(source, landing, small_sem).start()
 
     barrier = pltpu.get_barrier_semaphore()
     partners = [(0, dx, dy) for dx, dy in AROUND] + [(-1, 0, 0), (1, 0, 0)]
@@ -103,42 +101,38 @@
         for dx, dy in moves:
             guarded(there(-dz, -dx, -dy), lambda move=(dx, dy): copies[move].wait_recv())
 
-    def remote(source, landing, out_sem, in_sem, move):
+    def remote(source, landing, in_sem, move):
         return pltpu.make_async_remote_copy(
             src_ref=source, dst_ref=landing, send_sem=out_sem, recv_sem=in_sem,
             device_id=target(*move), device_id_type=pl.DeviceIdType.MESH,
         )
 
-    def index_of(move):
-        return (move[0] + 1) * 3 + move[1] + 1
-
     fine_copies = {}
     for move in AROUND:
         dx, dy = move
-        k = index_of(move)
         if dy == 0:
             continue
+        k = y_moves.index(move)
         if dx == 0:
             source, landing = y_send.at[(dy + 1) // 2], y_recv.at[(1 - dy) // 2]
         else:
             source = y_send.at[(dy + 1) // 2, pl.ds(0 if dx < 0 else part - REACH, REACH)]
             landing = corner_recv.at[(1 - dx) // 2, (1 - dy) // 2]
-        fine_copies[move] = remote(source, landing, fine_out.at[k], fine_in.at[k], (0, dx, dy))
+        fine_copies[move] = remote(source, landing, fine_in.at[k], (0, dx, dy))
     x_copies = []
     for r in range(REACH):
         copies = {}
         for dx in (-1, 1):
             towards = (dx + 1) // 2
-            k = towards * REACH + r
             source = x_hbm.at[:, r if dx < 0 else rows - REACH + r]
-            copies[dx, 0] = remote(source, x_recv.at[towards, r], x_out.at[k], x_in.at[k], (0, dx, 0))
+            copies[dx, 0] = remote(source, x_recv.at[towards, r], x_in.at[towards], (0, dx, 0))
         x_copies.append(copies)
 
-    def coarse_copies(main, wide_in, strips, out_sems, in_sems, dz):
+    def coarse_copies(main, wide_in, strips, in_sems, dz):
         row_out, row_in, side_out, side_in, corner_out, corner_in = strips
         copies = {}
         for dx, dy in PLANE if dz else AROUND:
-            k = index_of((dx, dy))
+            k = (PLANE if dz else AROUND).index((dx, dy))
             towards_x, towards_y = (dx + 1) // 2, (dy + 1) // 2
             if dx == 0 and dy == 0:
                 source, landing = main, wide_in.at[pl.ds(COARSE_REACH, part_c), pl.ds(FRONT, cols_c)]
@@ -148,12 +142,12 @@
                 source, landing = side_out.at[towards_y], side_in.at[towards_y]
             else:
                 source, landing = corner_out.at[towards_x, towards_y], corner_in.at[towards_x, towards_y]
-            copies[dx, dy] = remote(source, landing, out_sems.at[k], in_sems.at[k], (dz, dx, dy))
+            copies[dx, dy] = remote(source, landing, in_sems.at[k], (dz, dx, dy))
         return copies
 
     old_strips, new_strips = strip_refs[:6], strip_refs[6:]
-    old_copies = coarse_copies(None, old_wide, old_strips, old_out, old_in, 0)
-    chain_copies = coarse_copies(sent, new_wide, new_strips, chain_out, chain_in, 1)
+    old_copies = coarse_copies(None, old_wide, old_strips, old_in, 0)
+    chain_copies = coarse_copies(sent, new_wide, new_strips, chain_in, 1)
 
     lane = lax.broadcasted_iota(jnp.int32, (1, LANES), 1)
     pack = lane // levels
@@ -182,8 +176,6 @@
         stacked = jnp.concatenate([native_row(p * part + row - REACH) for p in range(packs)], axis=0)
         first[row, pl.ds(FRONT, cols), :] = stacked.T
 
-    x_moves = tuple(m for m in AROUND if m[1] == 0)
-    y_moves = tuple(m for m in AROUND if m[1] != 0)
     low_lanes = lane < levels
     high_lanes = lane >= LANES - levels
     pl.semaphore_wait(barrier, awaited)
@@ -192,15 +184,12 @@
     def _():
         pl.semaphore_signal(ready, inc=1, device_id=target(-1, 0, 0), device_id_type=pl.DeviceIdType.MESH)
 
-    side_moves = tuple(m for m in AROUND if m[0] == 0)
-    corner_moves = tuple(m for m in y_moves if m[0] != 0)
     for copies in x_copies[: REACH // 2]:
         send_all(copies, 0, x_moves)
-    for load in small_loads:
-        load.wait()
-    diffuse = packed(diff_ref[...])
-    east_wind = packed(wind_ref[0:1, :])
-    north_wind = packed(wind_ref[1:2, :])
+    pltpu.make_async_copy(small_ref, small_ref, small_sem).wait()
+    diffuse = packed(small_ref[0:1, :])
+    east_wind = packed(small_ref[1:2, :])
+    north_wind = packed(small_ref[2:3, :])
 
     def constants(factor):
         spread = (time_step * factor) * diffuse
@@ -209,9 +198,8 @@
     fine_constants = constants(1.0)
     coarse_constants = constants(0.25)
 
+    pltpu.make_async_copy(x_ref, x_ref, load_sem).wait()
     for row in range(REACH, REACH + part):
-        for p in range(packs):
-            loads[p * part + row - REACH].wait()
         bring_in(row)
     for row in range(part):
         y_send[0, row] = first[REACH + row, pl.ds(FRONT, REACH), :]
@@ -316,7 +304,6 @@
             extended[row, pl.ds(begin_c, count_c), :] = jnp.where(mask, value, 0.0)
 
     all_arrived(old_copies, 0, AROUND)
-    sends_done(old_copies, 0, AROUND)
     extend(old_wide, old_strips)
     for row in range(1, wide_c - 1):
         old_image[row - 1] = advance(extended, row, begin_c, count_c, coarse_constants)
@@ -344,8 +331,9 @@
         for row in range(part_c):
             sent[row] = smoothed(row)
 
-    for copies in x_copies:
-        all_arrived(copies, 0, x_moves)
+    for dx in (-1, 1):
+        whole = x_recv.at[(dx + 1) // 2]
+        guarded(there(0, -dx, 0), remote(whole, whole, x_in.at[(dx + 1) // 2], (0, dx, 0)).wait_recv)
     for row in halo_rows:
         bring_in(row)
         inner = first[row, pl.ds(FRONT, cols), :]
@@ -405,12 +393,13 @@
         pass_on()
 
     sends_done(fine_copies, 0, y_moves)
+    sends_done(old_copies, 0, AROUND)
     for copies in x_copies:
         sends_done(copies, 0, x_moves)
     pl.when(tm < n_tm - 1)(lambda: sends_done(chain_copies, 1, PLANE))
 
 
-def closing(levels, rows, turned, change, out_hbm, filled, spread_rows, sems):
+def closing(levels, rows, turned, change, out_hbm, filled, spread_rows, sem):
     packs = LANES // levels
     part, _, cols = turned.shape
     part_c = part // RATIO
@@ -436,7 +425,6 @@
 
     for row in range(2):
         spread_rows[row] = spread_row(row)
-    copies = []
     for row in range(part):
         at, o = row // RATIO, row % RATIO
         if o == 0:
@@ -449,11 +437,8 @@
         filled[row] = total
         for p in range(packs):
             x = p * part + row
-            copy = pltpu.make_async_copy(filled.at[row, pl.ds(p * levels, levels)], out_hbm.at[:, x], sems.at[x])
-            copy.start()
-            copies.append(copy)
-    for copy in copies:
-        copy.wait()
+            pltpu.make_async_copy(filled.at[row, pl.ds(p * levels, levels)], out_hbm.at[:, x], sem).start()
+    pltpu.make_async_copy(filled, filled, sem).wait()
 
 
 def shards(sizes, state_starts, diffusivity, wind):
@@ -468,10 +453,9 @@
     vmem = functools.partial(pltpu.VMEM, dtype=jnp.float32)
     scratch = [
         vmem((rows, levels, cols)),
-        vmem((1, levels)),
-        vmem((2, levels)),
-        pltpu.SemaphoreType.DMA((rows,)),
-        pltpu.SemaphoreType.DMA((2,)),
+        vmem((3, levels)),
+        pltpu.SemaphoreType.DMA,
+        pltpu.SemaphoreType.DMA,
         pltpu.SemaphoreType.REGULAR,
         vmem((wide, cols + 2 * FRONT, LANES)),
         vmem((wide, cols + 2 * FRONT, LANES)),
@@ -487,7 +471,8 @@
         vmem((part_c, cols_c, LANES)),
         vmem((cols_c + 2 * FRONT, LANES)),
         vmem((cols, LANES)),
-    ] + [pltpu.SemaphoreType.DMA((2 * REACH,))] * 2 + [pltpu.SemaphoreType.DMA((9,))] * 6
+        pltpu.SemaphoreType.DMA,
+    ] + [pltpu.SemaphoreType.DMA((count,)) for count in (2, len(y_moves), len(AROUND), len(PLANE))]
     scratch += [
         vmem((2, cols_c, LANES)),
         vmem((2, cols_c + 2 * FRONT, LANES)),
@@ -514,7 +499,7 @@
         scratch_shapes=[
             vmem((part, LANES, cols)),
             vmem((part_c + 2, LANES, cols)),
-            pltpu.SemaphoreType.DMA((rows,)),
+            pltpu.SemaphoreType.DMA,
         ],
         name="closing",
     )(*(pltpu.with_memory_space_constraint(array, pltpu.VMEM) for array in handed))

time: 23 us -> 21.1 us (0.917)
  Pallas kernels: 22.9 us -> 20.9 us
    pallas_call x1, Pallas kernels: 21.4 us -> 19.7 us  [shards(): pl.pallas_call(functools.partial(kernel, sizes, levels, rows, cols), out_...]
    pallas_call x1, Pallas kernels: 1.5 us -> 1.23 us  [shards(): pl.pallas_call(functools.partial(closing, levels, rows), out_shape=jax.Sh...]
where the time goes in v3:
time: 21.1 us; the launch traced here: 21 us
  Pallas kernels  20.9 us (99%)
    pallas_call x1, Pallas kernels, shards(): pl.pallas_call(functools.partial(kernel, sizes, levels, rows, cols), out_...  19.7 us
    pallas_call x1, Pallas kernels, shards(): pl.pallas_call(functools.partial(closing, levels, rows), out_shape=jax.Sh...  1.23 us

profile of v3, /device:TPU:24, one launch (start us, length us, event | category | flops | bytes accessed | tf_op | source)
XLA Modules:
  0.0 21.0 jit_solution(8264296825094695952)
XLA Ops:
  0.0 19.7 %parareal.1 = (f32[16,128,128]{2,1,0:T(8,128)S(1)}, f32[6,64,128]{2,1,0:T(8,128)S(1)}) custom-call(f32[64,32,128]{2,1,0:T(8,128)} %bitcast.3, f32[1,64]{1,0:T(1,128)} %bitcast.4, f32[2,64]{1,0:T(2,128)} %wind_hbm.1), custom_call_target="tpu_custom_call" | custom-call | tf_op jit(solution)/shard_map/parareal/pallas_call | solution.py:485
  19.7 1.2 %closing.1 = f32[64,32,128]{2,1,0:T(8,128)} custom-call(f32[16,128,128]{2,1,0:T(8,128)S(1)} %get-tuple-element.7.turned, f32[6,64,128]{2,1,0:T(8,128)S(1)} %get-tuple-element.8.change), custom_call_target="tpu_custom_call" | custom-call | tf_op jit(solution)/shard_map/closing/pallas_call | solution.py:494

commit v4 on v3

--- a/solution.py
+++ b/solution.py
@@ -39,11 +39,11 @@
 def kernel(
     sizes, levels, rows, cols,
     x_hbm, diff_hbm, wind_hbm, turned, change,
-    x_ref, small_ref, load_sem, small_sem, ready,
+    x_ref, small_ref, load_sems, small_sem, ready,
     first, second, x_recv, y_send, y_recv, corner_recv,
     old_wide, new_wide, extended, old_image,
     sent, fine_mean, line, fine_line,
-    out_sem, x_in, fine_in, old_in, chain_in, *strip_refs,
+    out_sem, near_in, far_in, fine_in, old_in, chain_in, *strip_refs,
 ):
     n_tm, n_gx, n_gy = sizes
     tm, gx, gy = lax.axis_index("tm"), lax.axis_index("gx"), lax.axis_index("gy")
@@ -74,8 +74,12 @@
     def target(dz, dx, dy):
         return (tm + dz, gx + dx, gy + dy)
 
-    for x in range(rows):
-        pltpu.make_async_copy(x_hbm.at[:, x], x_ref.at[x], load_sem).start()
+    rows_first = [*range(REACH), *range(part - REACH, part)]
+    rows_later = [*range(REACH, part - REACH)]
+    for group, group_rows in enumerate((rows_first, rows_later)):
+        for row in group_rows:
+            for x in range(row, rows, part):
+                pltpu.make_async_copy(x_hbm.at[:, x], x_ref.at[x], load_sems.at[group]).start()
     for source, landing in ((diff_hbm, small_ref.at[pl.ds(0, 1)]), (wind_hbm, small_ref.at[pl.ds(1, 2)])):
         pltpu.make_async_copy(source, landing, small_sem).start()
 
@@ -108,31 +112,29 @@
         )
 
     fine_copies = {}
-    for move in AROUND:
+    for move in y_moves:
         dx, dy = move
-        if dy == 0:
-            continue
-        k = y_moves.index(move)
         if dx == 0:
             source, landing = y_send.at[(dy + 1) // 2], y_recv.at[(1 - dy) // 2]
         else:
             source = y_send.at[(dy + 1) // 2, pl.ds(0 if dx < 0 else part - REACH, REACH)]
             landing = corner_recv.at[(1 - dx) // 2, (1 - dy) // 2]
-        fine_copies[move] = remote(source, landing, fine_in.at[k], (0, dx, dy))
-    x_copies = []
-    for r in range(REACH):
-        copies = {}
-        for dx in (-1, 1):
-            towards = (dx + 1) // 2
-            source = x_hbm.at[:, r if dx < 0 else rows - REACH + r]
-            copies[dx, 0] = remote(source, x_recv.at[towards, r], x_in.at[towards], (0, dx, 0))
-        x_copies.append(copies)
+        fine_copies[move] = remote(source, landing, fine_in.at[y_moves.index(move)], (0, dx, dy))
+    near, far = REACH // 2, REACH - REACH // 2
+    near_copies, far_copies = {}, {}
+    for dx in (-1, 1):
+        low = dx < 0
+        for copies, start, count, in_sems in (
+            (near_copies, 0 if low else far, near, near_in), (far_copies, near if low else 0, far, far_in)
+        ):
+            source = x_ref.at[pl.ds(start if low else rows - REACH + start, count)]
+            landing = x_recv.at[0 if low else 1, pl.ds(start, count)]
+            copies[dx, 0] = remote(source, landing, in_sems.at[0 if low else 1], (0, dx, 0))
 
     def coarse_copies(main, wide_in, strips, in_sems, dz):
         row_out, row_in, side_out, side_in, corner_out, corner_in = strips
         copies = {}
         for dx, dy in PLANE if dz else AROUND:
-            k = (PLANE if dz else AROUND).index((dx, dy))
             towards_x, towards_y = (dx + 1) // 2, (dy + 1) // 2
             if dx == 0 and dy == 0:
                 source, landing = main, wide_in.at[pl.ds(COARSE_REACH, part_c), pl.ds(FRONT, cols_c)]
@@ -142,6 +144,7 @@
                 source, landing = side_out.at[towards_y], side_in.at[towards_y]
             else:
                 source, landing = corner_out.at[towards_x, towards_y], corner_in.at[towards_x, towards_y]
+            k = (PLANE if dz else AROUND).index((dx, dy))
             copies[dx, dy] = remote(source, landing, in_sems.at[k], (dz, dx, dy))
         return copies
 
@@ -184,8 +187,6 @@
     def _():
         pl.semaphore_signal(ready, inc=1, device_id=target(-1, 0, 0), device_id_type=pl.DeviceIdType.MESH)
 
-    for copies in x_copies[: REACH // 2]:
-        send_all(copies, 0, x_moves)
     pltpu.make_async_copy(small_ref, small_ref, small_sem).wait()
     diffuse = packed(small_ref[0:1, :])
     east_wind = packed(small_ref[1:2, :])
@@ -198,13 +199,23 @@
     fine_constants = constants(1.0)
     coarse_constants = constants(0.25)
 
-    pltpu.make_async_copy(x_ref, x_ref, load_sem).wait()
-    for row in range(REACH, REACH + part):
-        bring_in(row)
-    for row in range(part):
-        y_send[0, row] = first[REACH + row, pl.ds(FRONT, REACH), :]
-        y_send[1, row] = first[REACH + row, pl.ds(end - REACH, REACH), :]
-    send_all(fine_copies, 0, side_moves + corner_moves)
+    def load_done(group, group_rows):
+        whole = x_ref.at[pl.ds(0, packs * len(group_rows))]
+        pltpu.make_async_copy(whole, whole, load_sems.at[group]).wait()
+
+    def bring_own(group_rows):
+        for row in group_rows:
+            bring_in(REACH + row)
+            y_send[0, row] = first[REACH + row, pl.ds(FRONT, REACH), :]
+            y_send[1, row] = first[REACH + row, pl.ds(end - REACH, REACH), :]
+
+    load_done(0, rows_first)
+    bring_own(rows_first)
+    send_all(fine_copies, 0, corner_moves)
+    send_all(near_copies, 0, x_moves)
+    load_done(1, rows_later)
+    bring_own(rows_later)
+    send_all(fine_copies, 0, side_moves)
 
     def restricted(source, row):
         total = source[REACH + row * RATIO, pl.ds(FRONT, cols), :]
@@ -227,7 +238,7 @@
             for row in range(part_c):
                 side_out[side, pl.ds(COARSE_REACH * row, COARSE_REACH), :] = row_of(row, col, COARSE_REACH)
             for towards in range(2):
-                corner_out[towards, side, pl.ds(0, COARSE_REACH), :] = row_out[towards, pl.ds(col, COARSE_REACH), :]
+                corner_out[towards, side] = row_out[towards, pl.ds(col, COARSE_REACH), :]
 
     def old_row(row, col, count):
         return old_wide[COARSE_REACH + row, pl.ds(FRONT + col, count), :]
@@ -236,8 +247,7 @@
         old_wide[COARSE_REACH + row, pl.ds(FRONT, cols_c), :] = restricted(first, row)
     pack_strips(old_row, old_strips)
     send_all(old_copies, 0, AROUND)
-    for copies in x_copies[REACH // 2 :]:
-        send_all(copies, 0, x_moves)
+    send_all(far_copies, 0, x_moves)
 
     def inside_x(row, reach, length):
         place = (gx * packs + pack) * length + (row - reach)
@@ -249,28 +259,78 @@
 
     edges = ((FRONT - EDGE, inside_y(FRONT - EDGE, EDGE, cols)), (end, inside_y(end, EDGE, cols)))
     reaches = ((FRONT - REACH, inside_y(FRONT - REACH, REACH, cols)), (end, inside_y(end, REACH, cols)))
-    halo_rows = [*range(REACH), *range(REACH + part, wide)]
     half = cols // 2
+
+    def fill(source, dest, row, start, count, consts):
+        dest[row, pl.ds(start, count), :] = advance(source, row, start, count, consts)
+
+    def fill_edges(source, dest, row, consts):
+        for start, mask in edges:
+            value = advance(source, row, start, EDGE, consts)
+            dest[row, pl.ds(start, EDGE), :] = jnp.where(mask, value, 0.0)
 
     def update(source, dest, row, consts, last):
         for start, count in ((FRONT, half), (FRONT + half, cols - half)):
-            dest[row, pl.ds(start, count), :] = advance(source, row, start, count, consts)
+            fill(source, dest, row, start, count, consts)
         if not last:
-            for start, mask in edges:
-                value = advance(source, row, start, EDGE, consts)
-                dest[row, pl.ds(start, EDGE), :] = jnp.where(mask, value, 0.0)
+            fill_edges(source, dest, row, consts)
 
     buffers = (first, second)
 
+    def inner_steps(row_update):
+        for step in range(1, SUB + 1):
+            def inner_row(row, step=step):
+                row_update(buffers[(step - 1) % 2], buffers[step % 2], row, step)
+
+            pl.loop(REACH + step, REACH + part - step, unroll=2)(inner_row)
+
+    def centre_update(source, dest, row, step):
+        fill(source, dest, row, FRONT + EDGE * step, half - EDGE * step, fine_constants)
+        fill(source, dest, row, FRONT + half, cols - half - EDGE * step, fine_constants)
+
+    def sides_update(source, dest, row, step):
+        fill(source, dest, row, FRONT, EDGE * step, fine_constants)
+        fill(source, dest, row, end - EDGE * step, EDGE * step, fine_constants)
+        if step < SUB:
+            fill_edges(source, dest, row, fine_constants)
+
+    inner_steps(centre_update)
     all_arrived(fine_copies, 0, side_moves)
     for side, (start, mask) in enumerate(reaches):
         for row in range(part):
             first[REACH + row, pl.ds(start, REACH), :] = jnp.where(mask, y_recv[side, row], 0.0)
-    for step in range(1, SUB + 1):
-        def inner_row(row, step=step):
-            update(buffers[(step - 1) % 2], buffers[step % 2], row, fine_constants, step == SUB)
-
-        pl.loop(REACH + step, REACH + part - step, unroll=2)(inner_row)
+    inner_steps(sides_update)
+
+    def bring_halo(halo_rows):
+        for row in halo_rows:
+            bring_in(row)
+            inner = first[row, pl.ds(FRONT, cols), :]
+            first[row, pl.ds(FRONT, cols), :] = jnp.where(inside_x(row, REACH, part), inner, 0.0)
+        for side, (start, mask_side) in enumerate(reaches):
+            for row in halo_rows:
+                if row < REACH:
+                    here = jnp.where(high_lanes, corner_recv[0, side, row], y_recv[side, row + part - REACH])
+                    here = pltpu.roll(here, levels, 1)
+                else:
+                    at = row - part - REACH
+                    here = pltpu.roll(jnp.where(low_lanes, corner_recv[1, side, at], y_recv[side, at]), LANES - levels, 1)
+                mask = jnp.logical_and(mask_side, inside_x(row, REACH, part))
+                first[row, pl.ds(start, REACH), :] = jnp.where(mask, here, 0.0)
+
+    def outer_steps(low_shift, high_shift, count):
+        for step in range(1, SUB + 1):
+            def outer_row(k, step=step):
+                for row in (step + low_shift + k, part + REACH - step + high_shift + k):
+                    mask_x = inside_x(row, REACH, part)
+                    consts = tuple(jnp.where(mask_x, c, 0.0) for c in fine_constants)
+                    update(buffers[(step - 1) % 2], buffers[step % 2], row, consts, step == SUB)
+
+            pl.loop(0, count)(outer_row)
+
+    all_arrived(near_copies, 0, x_moves)
+    all_arrived(fine_copies, 0, corner_moves)
+    bring_halo([*range(far, REACH), *range(REACH + part, REACH + part + near)])
+    outer_steps(far, 0, near)
 
     count_c = cols_c + 2 * EDGE
     begin_c = FRONT - EDGE
@@ -284,7 +344,7 @@
                     side, pl.ds(COARSE_REACH * row, COARSE_REACH), :
                 ]
             for towards in range(2):
-                row_in[towards, pl.ds(col, COARSE_REACH), :] = corner_in[towards, side, pl.ds(0, COARSE_REACH), :]
+                row_in[towards, pl.ds(col, COARSE_REACH), :] = corner_in[towards, side]
 
         def own(row):
             return buffer[COARSE_REACH + row, pl.ds(begin_c, count_c), :]
@@ -331,32 +391,9 @@
         for row in range(part_c):
             sent[row] = smoothed(row)
 
-    for dx in (-1, 1):
-        whole = x_recv.at[(dx + 1) // 2]
-        guarded(there(0, -dx, 0), remote(whole, whole, x_in.at[(dx + 1) // 2], (0, dx, 0)).wait_recv)
-    for row in halo_rows:
-        bring_in(row)
-        inner = first[row, pl.ds(FRONT, cols), :]
-        first[row, pl.ds(FRONT, cols), :] = jnp.where(inside_x(row, REACH, part), inner, 0.0)
-    all_arrived(fine_copies, 0, corner_moves)
-    for side, (start, mask_side) in enumerate(reaches):
-        for row in halo_rows:
-            if row < REACH:
-                here = jnp.where(high_lanes, corner_recv[0, side, row], y_recv[side, row + part - REACH])
-                here = pltpu.roll(here, levels, 1)
-            else:
-                here = jnp.where(low_lanes, corner_recv[1, side, row - part - REACH], y_recv[side, row - part - REACH])
-                here = pltpu.roll(here, LANES - levels, 1)
-            mask = jnp.logical_and(mask_side, inside_x(row, REACH, part))
-            first[row, pl.ds(start, REACH), :] = jnp.where(mask, here, 0.0)
-    for step in range(1, SUB + 1):
-        def outer_row(row, step=step):
-            for shifted in (row, row + part + REACH - 2 * step):
-                mask_x = inside_x(shifted, REACH, part)
-                consts = tuple(jnp.where(mask_x, c, 0.0) for c in fine_constants)
-                update(buffers[(step - 1) % 2], buffers[step % 2], shifted, consts, step == SUB)
-
-        pl.loop(step, REACH + step)(outer_row)
+    all_arrived(far_copies, 0, x_moves)
+    bring_halo([*range(far), *range(REACH + part + near, wide)])
+    outer_steps(0, near, far)
     fine = buffers[SUB % 2]
 
     for row in range(part_c):
@@ -394,8 +431,8 @@
 
     sends_done(fine_copies, 0, y_moves)
     sends_done(old_copies, 0, AROUND)
-    for copies in x_copies:
-        sends_done(copies, 0, x_moves)
+    sends_done(near_copies, 0, x_moves)
+    sends_done(far_copies, 0, x_moves)
     pl.when(tm < n_tm - 1)(lambda: sends_done(chain_copies, 1, PLANE))
 
 
@@ -454,7 +491,7 @@
     scratch = [
         vmem((rows, levels, cols)),
         vmem((3, levels)),
-        pltpu.SemaphoreType.DMA,
+        pltpu.SemaphoreType.DMA((2,)),
         pltpu.SemaphoreType.DMA,
         pltpu.SemaphoreType.REGULAR,
         vmem((wide, cols + 2 * FRONT, LANES)),
@@ -472,14 +509,14 @@
         vmem((cols_c + 2 * FRONT, LANES)),
         vmem((cols, LANES)),
         pltpu.SemaphoreType.DMA,
-    ] + [pltpu.SemaphoreType.DMA((count,)) for count in (2, len(y_moves), len(AROUND), len(PLANE))]
+    ] + [pltpu.SemaphoreType.DMA((count,)) for count in (2, 2, len(y_moves), len(AROUND), len(PLANE))]
     scratch += [
         vmem((2, cols_c, LANES)),
         vmem((2, cols_c + 2 * FRONT, LANES)),
         vmem((2, COARSE_REACH * part_c, LANES)),
         vmem((2, COARSE_REACH * part_c, LANES)),
-        vmem((2, 2, EDGE, LANES)),
-        vmem((2, 2, EDGE, LANES)),
+        vmem((2, 2, COARSE_REACH, LANES)),
+        vmem((2, 2, COARSE_REACH, LANES)),
     ] * 2
     in_vmem = pl.BlockSpec(memory_space=pltpu.VMEM)
     handed = pl.pallas_call(

time: 21.1 us -> 20.2 us (0.957)
  Pallas kernels: 20.9 us -> 20 us
    pallas_call x1, Pallas kernels: 19.7 us -> 18.8 us  [shards(): pl.pallas_call(functools.partial(kernel, sizes, levels, rows, cols), out_...]
where the time goes in v4:
time: 20.2 us; the launch traced here: 20 us
  Pallas kernels  20 us (99%)
    pallas_call x1, Pallas kernels, shards(): pl.pallas_call(functools.partial(kernel, sizes, levels, rows, cols), out_...  18.8 us
    pallas_call x1, Pallas kernels, shards(): pl.pallas_call(functools.partial(closing, levels, rows), out_shape=jax.Sh...  1.22 us

profile of v4, /device:TPU:24, one launch (start us, length us, event | category | flops | bytes accessed | tf_op | source)
XLA Modules:
  0.0 20.0 jit_solution(7896043412918607765)
XLA Ops:
  0.0 18.8 %parareal.1 = (f32[16,128,128]{2,1,0:T(8,128)S(1)}, f32[6,64,128]{2,1,0:T(8,128)S(1)}) custom-call(f32[64,32,128]{2,1,0:T(8,128)} %bitcast.3, f32[1,64]{1,0:T(1,128)} %bitcast.4, f32[2,64]{1,0:T(2,128)} %wind_hbm.1), custom_call_target="tpu_custom_call" | custom-call | tf_op jit(solution)/shard_map/parareal/pallas_call | solution.py:522
  18.8 1.2 %closing.1 = f32[64,32,128]{2,1,0:T(8,128)} custom-call(f32[16,128,128]{2,1,0:T(8,128)S(1)} %get-tuple-element.7.turned, f32[6,64,128]{2,1,0:T(8,128)S(1)} %get-tuple-element.8.change), custom_call_target="tpu_custom_call" | custom-call | tf_op jit(solution)/shard_map/closing/pallas_call | solution.py:531

commit v5 on v4

--- a/solution.py
+++ b/solution.py
@@ -1,4 +1,5 @@
 import functools
+import math
 
 import jax
 import jax.numpy as jnp
@@ -14,6 +15,7 @@
 EDGE = 8
 FRONT = 2 * EDGE
 COARSE_REACH = 2
+TALLY = 1024
 
 time_step = 0.2
 weights_low = (0.375, 0.125, 0.0, 0.0)
@@ -42,8 +44,8 @@
     x_ref, small_ref, load_sems, small_sem, ready,
     first, second, x_recv, y_send, y_recv, corner_recv,
     old_wide, new_wide, extended, old_image,
-    sent, fine_mean, line, fine_line,
-    out_sem, near_in, far_in, fine_in, old_in, chain_in, *strip_refs,
+    sent, fine_mean, line, fine_line, tally,
+    out_sem, near_in, far_in, side_in_sem, corner_in_sem, old_in, chain_in, *strip_refs,
 ):
     n_tm, n_gx, n_gy = sizes
     tm, gx, gy = lax.axis_index("tm"), lax.axis_index("gx"), lax.axis_index("gy")
@@ -101,9 +103,23 @@
         for move in moves:
             guarded(there(dz, *move), lambda move=move: copies[move].wait_send())
 
-    def all_arrived(copies, dz, moves):
+    stand_ins, sizes_in_rows = {}, {}
+
+    def fill_missing(copies, moves):
         for dx, dy in moves:
-            guarded(there(-dz, -dx, -dy), lambda move=(dx, dy): copies[move].wait_recv())
+            @pl.when(jnp.logical_not(there(0, -dx, -dy)))
+            def _(dx=dx, dy=dy):
+                pltpu.make_async_copy(*stand_ins[id(copies)][dx, dy]).start()
+
+    def all_arrived(copies, in_sem, moves):
+        height = sum(sizes_in_rows[id(copies)][move] for move in moves)
+        whole = tally.at[pl.ds(0, height)]
+        pltpu.make_async_copy(whole, whole, in_sem).wait()
+
+    def plan(copies, move, source, landing, in_sem, dz=0):
+        copies[move] = remote(source, landing, in_sem, (dz, *move))
+        stand_ins.setdefault(id(copies), {})[move] = (source, landing, in_sem)
+        sizes_in_rows.setdefault(id(copies), {})[move] = math.prod(source.shape[:-1])
 
     def remote(source, landing, in_sem, move):
         return pltpu.make_async_remote_copy(
@@ -115,23 +131,23 @@
     for move in y_moves:
         dx, dy = move
         if dx == 0:
-            source, landing = y_send.at[(dy + 1) // 2], y_recv.at[(1 - dy) // 2]
+            source, landing, in_sem = y_send.at[(dy + 1) // 2], y_recv.at[(1 - dy) // 2], side_in_sem
         else:
             source = y_send.at[(dy + 1) // 2, pl.ds(0 if dx < 0 else part - REACH, REACH)]
-            landing = corner_recv.at[(1 - dx) // 2, (1 - dy) // 2]
-        fine_copies[move] = remote(source, landing, fine_in.at[y_moves.index(move)], (0, dx, dy))
+            landing, in_sem = corner_recv.at[(1 - dx) // 2, (1 - dy) // 2], corner_in_sem
+        plan(fine_copies, move, source, landing, in_sem)
     near, far = REACH // 2, REACH - REACH // 2
     near_copies, far_copies = {}, {}
     for dx in (-1, 1):
         low = dx < 0
-        for copies, start, count, in_sems in (
+        for copies, start, count, in_sem in (
             (near_copies, 0 if low else far, near, near_in), (far_copies, near if low else 0, far, far_in)
         ):
             source = x_ref.at[pl.ds(start if low else rows - REACH + start, count)]
             landing = x_recv.at[0 if low else 1, pl.ds(start, count)]
-            copies[dx, 0] = remote(source, landing, in_sems.at[0 if low else 1], (0, dx, 0))
-
-    def coarse_copies(main, wide_in, strips, in_sems, dz):
+            plan(copies, (dx, 0), source, landing, in_sem)
+
+    def coarse_copies(main, wide_in, strips, in_sem, dz):
         row_out, row_in, side_out, side_in, corner_out, corner_in = strips
         copies = {}
         for dx, dy in PLANE if dz else AROUND:
@@ -144,8 +160,7 @@
                 source, landing = side_out.at[towards_y], side_in.at[towards_y]
             else:
                 source, landing = corner_out.at[towards_x, towards_y], corner_in.at[towards_x, towards_y]
-            k = (PLANE if dz else AROUND).index((dx, dy))
-            copies[dx, dy] = remote(source, landing, in_sems.at[k], (dz, dx, dy))
+            plan(copies, (dx, dy), source, landing, in_sem, dz)
         return copies
 
     old_strips, new_strips = strip_refs[:6], strip_refs[6:]
@@ -294,8 +309,13 @@
         if step < SUB:
             fill_edges(source, dest, row, fine_constants)
 
+    fill_missing(fine_copies, side_moves)
+    fill_missing(fine_copies, corner_moves)
+    fill_missing(near_copies, x_moves)
+    fill_missing(far_copies, x_moves)
+    fill_missing(old_copies, AROUND)
     inner_steps(centre_update)
-    all_arrived(fine_copies, 0, side_moves)
+    all_arrived(fine_copies, side_in_sem, side_moves)
     for side, (start, mask) in enumerate(reaches):
         for row in range(part):
             first[REACH + row, pl.ds(start, REACH), :] = jnp.where(mask, y_recv[side, row], 0.0)
@@ -327,8 +347,8 @@
 
             pl.loop(0, count)(outer_row)
 
-    all_arrived(near_copies, 0, x_moves)
-    all_arrived(fine_copies, 0, corner_moves)
+    all_arrived(near_copies, near_in, x_moves)
+    all_arrived(fine_copies, corner_in_sem, corner_moves)
     bring_halo([*range(far, REACH), *range(REACH + part, REACH + part + near)])
     outer_steps(far, 0, near)
 
@@ -363,7 +383,7 @@
                 mask = jnp.logical_and(mask_y, inside_x(row, COARSE_REACH, part_c))
             extended[row, pl.ds(begin_c, count_c), :] = jnp.where(mask, value, 0.0)
 
-    all_arrived(old_copies, 0, AROUND)
+    all_arrived(old_copies, old_in, AROUND)
     extend(old_wide, old_strips)
     for row in range(1, wide_c - 1):
         old_image[row - 1] = advance(extended, row, begin_c, count_c, coarse_constants)
@@ -391,7 +411,7 @@
         for row in range(part_c):
             sent[row] = smoothed(row)
 
-    all_arrived(far_copies, 0, x_moves)
+    all_arrived(far_copies, far_in, x_moves)
     bring_halo([*range(far), *range(REACH + part + near, wide)])
     outer_steps(0, near, far)
     fine = buffers[SUB % 2]
@@ -415,11 +435,15 @@
             sent[row] = fine_mean[row] + sent[row]
         pass_on()
 
-    write_fine()
-
     @pl.when(tm > 0)
     def _():
-        all_arrived(chain_copies, 1, PLANE)
+        fill_missing(chain_copies, AROUND)
+
+    write_fine()
+
+    @pl.when(tm > 0)
+    def _():
+        all_arrived(chain_copies, chain_in, PLANE)
         extend(new_wide, new_strips)
         compute_change()
 
@@ -508,8 +532,8 @@
         vmem((part_c, cols_c, LANES)),
         vmem((cols_c + 2 * FRONT, LANES)),
         vmem((cols, LANES)),
-        pltpu.SemaphoreType.DMA,
-    ] + [pltpu.SemaphoreType.DMA((count,)) for count in (2, 2, len(y_moves), len(AROUND), len(PLANE))]
+        vmem((TALLY, LANES)),
+    ] + [pltpu.SemaphoreType.DMA] * 7
     scratch += [
         vmem((2, cols_c, LANES)),
         vmem((2, cols_c + 2 * FRONT, LANES)),

time: 20.2 us -> 20 us (0.990)
  no operation moved by 1% of the time
where the time goes in v5:
time: 20 us; the launch traced here: 19.8 us
  Pallas kernels  19.8 us (99%)
    pallas_call x1, Pallas kernels, shards(): pl.pallas_call(functools.partial(kernel, sizes, levels, rows, cols), out_...  18.6 us
    pallas_call x1, Pallas kernels, shards(): pl.pallas_call(functools.partial(closing, levels, rows), out_shape=jax.Sh...  1.23 us

profile of v5, /device:TPU:24, one launch (start us, length us, event | category | flops | bytes accessed | tf_op | source)
XLA Modules:
  0.0 19.8 jit_solution(11116426255487504738)
XLA Ops:
  0.0 18.6 %parareal.1 = (f32[16,128,128]{2,1,0:T(8,128)S(1)}, f32[6,64,128]{2,1,0:T(8,128)S(1)}) custom-call(f32[64,32,128]{2,1,0:T(8,128)} %bitcast.3, f32[1,64]{1,0:T(1,128)} %bitcast.4, f32[2,64]{1,0:T(2,128)} %wind_hbm.1), custom_call_target="tpu_custom_call" | custom-call | tf_op jit(solution)/shard_map/parareal/pallas_call | solution.py:546
  18.6 1.2 %closing.1 = f32[64,32,128]{2,1,0:T(8,128)} custom-call(f32[16,128,128]{2,1,0:T(8,128)S(1)} %get-tuple-element.7.turned, f32[6,64,128]{2,1,0:T(8,128)S(1)} %get-tuple-element.8.change), custom_call_target="tpu_custom_call" | custom-call | tf_op jit(solution)/shard_map/closing/pallas_call | solution.py:555

commit v6 on v5

--- a/solution.py
+++ b/solution.py
@@ -15,6 +15,7 @@
 EDGE = 8
 FRONT = 2 * EDGE
 COARSE_REACH = 2
+LONG_REACH = 2 * COARSE_REACH
 TALLY = 1024
 
 time_step = 0.2
@@ -43,9 +44,9 @@
     x_hbm, diff_hbm, wind_hbm, turned, change,
     x_ref, small_ref, load_sems, small_sem, ready,
     first, second, x_recv, y_send, y_recv, corner_recv,
-    old_wide, new_wide, extended, old_image,
+    old_own, new_own, prior_old_own, prior_new_own, extended, long_extended, old_image, prior_image, prior_change, lift,
     sent, fine_mean, line, fine_line, tally,
-    out_sem, near_in, far_in, side_in_sem, corner_in_sem, old_in, chain_in, *strip_refs,
+    out_sem, near_in, far_in, side_in_sem, corner_in_sem, old_in, chain_in, prior_old_in, prior_new_in, *strip_refs,
 ):
     n_tm, n_gx, n_gy = sizes
     tm, gx, gy = lax.axis_index("tm"), lax.axis_index("gx"), lax.axis_index("gy")
@@ -62,9 +63,9 @@
         tests = []
         for place, move, count in ((tm, dz, n_tm), (gx, dx, n_gx), (gy, dy, n_gy)):
             if move < 0:
-                tests.append(place > 0)
+                tests.append(place >= -move)
             if move > 0:
-                tests.append(place < count - 1)
+                tests.append(place < count - move)
         return conjunction(tests)
 
     def guarded(condition, action):
@@ -86,14 +87,16 @@
         pltpu.make_async_copy(source, landing, small_sem).start()
 
     barrier = pltpu.get_barrier_semaphore()
-    partners = [(0, dx, dy) for dx, dy in AROUND] + [(-1, 0, 0), (1, 0, 0)]
+    odd = tm % 2 == 1
+    partners = [(0, dx, dy) for dx, dy in AROUND] + [(dz, 0, 0) for dz in (-1, 1, -2, 2)]
     partners.sort(key=lambda move: -sum(map(abs, move)))
     awaited = jnp.int32(0)
     for move in partners:
         def greet(move=move):
             pl.semaphore_signal(barrier, inc=1, device_id=target(*move), device_id_type=pl.DeviceIdType.MESH)
-        guarded(there(*move), greet)
-        awaited = awaited + there(*move).astype(jnp.int32)
+        met = jnp.logical_and(odd, there(*move)) if abs(move[0]) == 2 else there(*move)
+        guarded(met, greet)
+        awaited = awaited + met.astype(jnp.int32)
 
     def send_all(copies, dz, moves):
         for move in moves:
@@ -147,15 +150,15 @@
             landing = x_recv.at[0 if low else 1, pl.ds(start, count)]
             plan(copies, (dx, 0), source, landing, in_sem)
 
-    def coarse_copies(main, wide_in, strips, in_sem, dz):
+    def coarse_copies(main, own_in, strips, in_sem, dz):
         row_out, row_in, side_out, side_in, corner_out, corner_in = strips
         copies = {}
         for dx, dy in PLANE if dz else AROUND:
             towards_x, towards_y = (dx + 1) // 2, (dy + 1) // 2
             if dx == 0 and dy == 0:
-                source, landing = main, wide_in.at[pl.ds(COARSE_REACH, part_c), pl.ds(FRONT, cols_c)]
+                source, landing = main, own_in.at[:, pl.ds(FRONT, cols_c)]
             elif dy == 0:
-                source, landing = row_out.at[towards_x], row_in.at[towards_x, pl.ds(FRONT, cols_c)]
+                source, landing = row_out.at[towards_x], row_in.at[towards_x, :, pl.ds(FRONT, cols_c)]
             elif dx == 0:
                 source, landing = side_out.at[towards_y], side_in.at[towards_y]
             else:
@@ -163,9 +166,13 @@
             plan(copies, (dx, dy), source, landing, in_sem, dz)
         return copies
 
-    old_strips, new_strips = strip_refs[:6], strip_refs[6:]
-    old_copies = coarse_copies(None, old_wide, old_strips, old_in, 0)
-    chain_copies = coarse_copies(sent, new_wide, new_strips, chain_in, 1)
+    old_strips, new_strips, prior_old_strips, prior_new_strips = (strip_refs[6 * k : 6 * k + 6] for k in range(4))
+    old_main = old_own.at[:, pl.ds(FRONT, cols_c)]
+    old_copies = coarse_copies(None, old_own, old_strips, old_in, 0)
+    chain_copies = coarse_copies(sent, new_own, new_strips, chain_in, 1)
+    prior_old_copies = coarse_copies(old_main, prior_old_own, prior_old_strips, prior_old_in, 1)
+    prior_new_copies = coarse_copies(sent, prior_new_own, prior_new_strips, prior_new_in, 2)
+    has_next, has_second = tm < n_tm - 1, tm < n_tm - 2
 
     lane = lax.broadcasted_iota(jnp.int32, (1, LANES), 1)
     pack = lane // levels
@@ -202,6 +209,10 @@
     def _():
         pl.semaphore_signal(ready, inc=1, device_id=target(-1, 0, 0), device_id_type=pl.DeviceIdType.MESH)
 
+    @pl.when(jnp.logical_and(odd, tm > 1))
+    def _():
+        pl.semaphore_signal(ready, inc=1, device_id=target(-2, 0, 0), device_id_type=pl.DeviceIdType.MESH)
+
     pltpu.make_async_copy(small_ref, small_ref, small_sem).wait()
     diffuse = packed(small_ref[0:1, :])
     east_wind = packed(small_ref[1:2, :])
@@ -228,6 +239,7 @@
     bring_own(rows_first)
     send_all(fine_copies, 0, corner_moves)
     send_all(near_copies, 0, x_moves)
+    send_all(far_copies, 0, x_moves)
     load_done(1, rows_later)
     bring_own(rows_later)
     send_all(fine_copies, 0, side_moves)
@@ -245,24 +257,29 @@
     def swapped(value):
         return pltpu.roll(value, levels, 1)
 
-    def pack_strips(row_of, strips):
+    def pack_strips(row_of, strips, reach):
         row_out, _, side_out, _, corner_out, _ = strips
-        row_out[0] = jnp.where(low_lanes, row_of(0, 0, cols_c), swapped(row_of(1, 0, cols_c)))
-        row_out[1] = jnp.where(low_lanes, swapped(row_of(part_c - 2, 0, cols_c)), row_of(part_c - 1, 0, cols_c))
-        for side, col in ((0, 0), (1, cols_c - COARSE_REACH)):
+        for k in range(reach // 2):
+            after, before = 2 * k, part_c - 2 * k - 2
+            row_out[0, k] = jnp.where(low_lanes, row_of(after, 0, cols_c), swapped(row_of(after + 1, 0, cols_c)))
+            row_out[1, k] = jnp.where(low_lanes, swapped(row_of(before, 0, cols_c)), row_of(before + 1, 0, cols_c))
+        for side, col in ((0, 0), (1, cols_c - reach)):
             for row in range(part_c):
-                side_out[side, pl.ds(COARSE_REACH * row, COARSE_REACH), :] = row_of(row, col, COARSE_REACH)
+                side_out[side, row] = row_of(row, col, reach)
             for towards in range(2):
-                corner_out[towards, side] = row_out[towards, pl.ds(col, COARSE_REACH), :]
+                for k in range(reach // 2):
+                    corner_out[towards, side, k] = row_out[towards, k, pl.ds(col, reach), :]
 
     def old_row(row, col, count):
-        return old_wide[COARSE_REACH + row, pl.ds(FRONT + col, count), :]
+        return old_own[row, pl.ds(FRONT + col, count), :]
+
+    def sent_row(row, col, count):
+        return sent[row, pl.ds(col, count), :]
 
     for row in range(part_c):
-        old_wide[COARSE_REACH + row, pl.ds(FRONT, cols_c), :] = restricted(first, row)
-    pack_strips(old_row, old_strips)
+        old_own[row, pl.ds(FRONT, cols_c), :] = restricted(first, row)
+    pack_strips(old_row, old_strips, COARSE_REACH)
     send_all(old_copies, 0, AROUND)
-    send_all(far_copies, 0, x_moves)
 
     def inside_x(row, reach, length):
         place = (gx * packs + pack) * length + (row - reach)
@@ -320,6 +337,16 @@
         for row in range(part):
             first[REACH + row, pl.ds(start, REACH), :] = jnp.where(mask, y_recv[side, row], 0.0)
     inner_steps(sides_update)
+
+    @pl.when(odd)
+    def _():
+        fill_missing(prior_old_copies, AROUND)
+
+    @pl.when(jnp.logical_and(jnp.logical_not(odd), has_next))
+    def _():
+        pl.semaphore_wait(ready, 1)
+        pack_strips(old_row, prior_old_strips, LONG_REACH)
+        send_all(prior_old_copies, 1, PLANE)
 
     def bring_halo(halo_rows):
         for row in halo_rows:
@@ -352,65 +379,6 @@
     bring_halo([*range(far, REACH), *range(REACH + part, REACH + part + near)])
     outer_steps(far, 0, near)
 
-    count_c = cols_c + 2 * EDGE
-    begin_c = FRONT - EDGE
-    mask_y = inside_y(begin_c, count_c, cols_c)
-
-    def extend(buffer, strips):
-        _, row_in, _, side_in, _, corner_in = strips
-        for side, col in ((0, end_c), (1, FRONT - COARSE_REACH)):
-            for row in range(part_c):
-                buffer[COARSE_REACH + row, pl.ds(col, COARSE_REACH), :] = side_in[
-                    side, pl.ds(COARSE_REACH * row, COARSE_REACH), :
-                ]
-            for towards in range(2):
-                row_in[towards, pl.ds(col, COARSE_REACH), :] = corner_in[towards, side]
-
-        def own(row):
-            return buffer[COARSE_REACH + row, pl.ds(begin_c, count_c), :]
-
-        above, below = (row_in[towards, pl.ds(begin_c, count_c), :] for towards in (0, 1))
-        values = [
-            jnp.where(low_lanes, below, swapped(own(part_c - 2))),
-            swapped(jnp.where(high_lanes, below, own(part_c - 1))),
-            *[own(row) for row in range(part_c)],
-            swapped(jnp.where(low_lanes, above, own(0))),
-            jnp.where(high_lanes, above, swapped(own(1))),
-        ]
-        for row, value in enumerate(values):
-            mask = mask_y
-            if not COARSE_REACH <= row < COARSE_REACH + part_c:
-                mask = jnp.logical_and(mask_y, inside_x(row, COARSE_REACH, part_c))
-            extended[row, pl.ds(begin_c, count_c), :] = jnp.where(mask, value, 0.0)
-
-    all_arrived(old_copies, old_in, AROUND)
-    extend(old_wide, old_strips)
-    for row in range(1, wide_c - 1):
-        old_image[row - 1] = advance(extended, row, begin_c, count_c, coarse_constants)
-
-
-    def compute_change():
-        for row in range(1, wide_c - 1):
-            moved = advance(extended, row, begin_c, count_c, coarse_constants) - old_image[row - 1]
-            mask = jnp.logical_and(mask_y, inside_x(row, COARSE_REACH, part_c))
-            change[row - 1, pl.ds(begin_c, count_c), :] = jnp.where(mask, moved, 0.0)
-
-    def change_row(row):
-        return change[row, pl.ds(begin_c, count_c), :]
-
-    def smoothed(row):
-        line[pl.ds(begin_c, count_c), :] = (
-            mean_side * (change_row(row) + change_row(row + 2)) + mean_mid * change_row(row + 1)
-        )
-        sides = line[pl.ds(FRONT - 1, cols_c), :] + line[pl.ds(FRONT + 1, cols_c), :]
-        return mean_side * sides + mean_mid * line[pl.ds(FRONT, cols_c), :]
-
-    @pl.when(tm == 0)
-    def _():
-        compute_change()
-        for row in range(part_c):
-            sent[row] = smoothed(row)
-
     all_arrived(far_copies, far_in, x_moves)
     bring_halo([*range(far), *range(REACH + part + near, wide)])
     outer_steps(0, near, far)
@@ -419,45 +387,136 @@
     for row in range(part_c):
         fine_mean[row] = restricted(fine, row)
 
-    def write_fine():
-        for row in range(part):
-            turned[row] = fine[REACH + row, pl.ds(FRONT, cols), :].T
-
-    def pass_on():
-        pl.semaphore_wait(ready, 1)
-        pack_strips(lambda row, col, count: sent[row, pl.ds(col, count), :], new_strips)
+    @pl.when(jnp.logical_and(jnp.logical_not(odd), has_next))
+    def _():
+        for row in range(part_c):
+            sent[row] = fine_mean[row]
+        pack_strips(sent_row, new_strips, COARSE_REACH)
         send_all(chain_copies, 1, AROUND)
         send_all(chain_copies, 1, ((0, 0),))
 
-    @pl.when(jnp.logical_and(tm == 0, tm < n_tm - 1))
+    count_c = cols_c + 2 * EDGE
+    begin_c = FRONT - EDGE
+    across = pl.ds(begin_c, count_c)
+    mask_y = inside_y(begin_c, count_c, cols_c)
+
+    def extend(buffer, strips, target, reach):
+        _, row_in, _, side_in, _, corner_in = strips
+        for side, col in ((0, end_c), (1, FRONT - reach)):
+            for row in range(part_c):
+                buffer[row, pl.ds(col, reach), :] = side_in[side, row]
+            for towards in range(2):
+                for k in range(reach // 2):
+                    row_in[towards, k, pl.ds(col, reach), :] = corner_in[towards, side, k]
+
+        def own(row):
+            return buffer[row, across, :]
+
+        values = [own(row) for row in range(part_c)]
+        for k in range(reach // 2):
+            above, below = (row_in[towards, k, across, :] for towards in (0, 1))
+            after, before = 2 * k, part_c - 2 * k - 2
+            values = [
+                jnp.where(low_lanes, below, swapped(own(before))),
+                swapped(jnp.where(high_lanes, below, own(before + 1))),
+                *values,
+                swapped(jnp.where(low_lanes, above, own(after))),
+                jnp.where(high_lanes, above, swapped(own(after + 1))),
+            ]
+        for row, value in enumerate(values):
+            mask = mask_y
+            if not reach <= row < reach + part_c:
+                mask = jnp.logical_and(mask_y, inside_x(row, reach, part_c))
+            target[row, across, :] = jnp.where(mask, value, 0.0)
+
+    def image_of(source, image):
+        for row in range(image.shape[0]):
+            image[row] = advance(source, row + 1, begin_c, count_c, coarse_constants)
+
+    def change_of(source, image, reach, result):
+        for row in range(image.shape[0]):
+            moved = advance(source, row + 1, begin_c, count_c, coarse_constants) - image[row]
+            mask = jnp.logical_and(mask_y, inside_x(row + 1, reach, part_c))
+            result[row, across, :] = jnp.where(mask, moved, 0.0)
+
+    def smoothed(source, row, start, count):
+        line[across, :] = (
+            mean_side * (source[row, across, :] + source[row + 2, across, :]) + mean_mid * source[row + 1, across, :]
+        )
+        sides = line[pl.ds(start - 1, count), :] + line[pl.ds(start + 1, count), :]
+        return mean_side * sides + mean_mid * line[pl.ds(start, count), :]
+
+    def find_lift():
+        change_of(long_extended, prior_image, LONG_REACH, prior_change)
+        for row in range(wide_c):
+            mask = jnp.logical_and(mask_y, inside_x(row, COARSE_REACH, part_c))
+            lift[row] = jnp.where(mask, smoothed(prior_change, row, begin_c, count_c), 0.0)
+
+    all_arrived(old_copies, old_in, AROUND)
+    extend(old_own, old_strips, extended, COARSE_REACH)
+    image_of(extended, old_image)
+    pl.when(tm == 0)(lambda: change_of(extended, old_image, COARSE_REACH, change))
+
+    @pl.when(tm > 0)
+    def _():
+        fill_missing(chain_copies, AROUND)
+
+    @pl.when(jnp.logical_and(odd, tm > 1))
+    def _():
+        fill_missing(prior_new_copies, AROUND)
+
+    @pl.when(odd)
+    def _():
+        all_arrived(prior_old_copies, prior_old_in, PLANE)
+        extend(prior_old_own, prior_old_strips, long_extended, LONG_REACH)
+        image_of(long_extended, prior_image)
+
+    pl.when(tm == 1)(find_lift)
+
+    for row in range(part):
+        turned[row] = fine[REACH + row, pl.ds(FRONT, cols), :].T
+
+    @pl.when(tm > 0)
+    def _():
+        all_arrived(chain_copies, chain_in, PLANE)
+        extend(new_own, new_strips, extended, COARSE_REACH)
+
+    @pl.when(jnp.logical_and(odd, tm > 1))
+    def _():
+        all_arrived(prior_new_copies, prior_new_in, PLANE)
+        extend(prior_new_own, prior_new_strips, long_extended, LONG_REACH)
+        find_lift()
+
+    @pl.when(odd)
+    def _():
+        for row in range(wide_c):
+            extended[row, across, :] = extended[row, across, :] + lift[row]
+
+    pl.when(tm > 0)(lambda: change_of(extended, old_image, COARSE_REACH, change))
+
+    @pl.when(jnp.logical_and(odd, has_next))
     def _():
         for row in range(part_c):
-            sent[row] = fine_mean[row] + sent[row]
-        pass_on()
-
-    @pl.when(tm > 0)
-    def _():
-        fill_missing(chain_copies, AROUND)
-
-    write_fine()
-
-    @pl.when(tm > 0)
-    def _():
-        all_arrived(chain_copies, chain_in, PLANE)
-        extend(new_wide, new_strips)
-        compute_change()
-
-    @pl.when(jnp.logical_and(tm > 0, tm < n_tm - 1))
-    def _():
-        for row in range(part_c):
-            sent[row] = fine_mean[row] + smoothed(row)
-        pass_on()
+            sent[row] = fine_mean[row] + smoothed(change, row, FRONT, cols_c)
+        pl.semaphore_wait(ready, 1 + has_second.astype(jnp.int32))
+
+        @pl.when(has_second)
+        def _():
+            pack_strips(sent_row, prior_new_strips, LONG_REACH)
+            send_all(prior_new_copies, 2, AROUND)
+            send_all(prior_new_copies, 2, ((0, 0),))
+
+        pack_strips(sent_row, new_strips, COARSE_REACH)
+        send_all(chain_copies, 1, AROUND)
+        send_all(chain_copies, 1, ((0, 0),))
 
     sends_done(fine_copies, 0, y_moves)
     sends_done(old_copies, 0, AROUND)
     sends_done(near_copies, 0, x_moves)
     sends_done(far_copies, 0, x_moves)
-    pl.when(tm < n_tm - 1)(lambda: sends_done(chain_copies, 1, PLANE))
+    pl.when(has_next)(lambda: sends_done(chain_copies, 1, PLANE))
+    pl.when(jnp.logical_and(jnp.logical_not(odd), has_next))(lambda: sends_done(prior_old_copies, 1, PLANE))
+    pl.when(jnp.logical_and(odd, has_second))(lambda: sends_done(prior_new_copies, 2, PLANE))
 
 
 def closing(levels, rows, turned, change, out_hbm, filled, spread_rows, sem):
@@ -510,7 +569,9 @@
     part = rows // packs
     part_c = part // RATIO
     cols_c = cols // RATIO
-    wide, wide_c = part + 2 * REACH, part_c + 2 * COARSE_REACH
+    wide, wide_c, wide_long = part + 2 * REACH, part_c + 2 * COARSE_REACH, part_c + 2 * LONG_REACH
+    if part_c < LONG_REACH:
+        raise ValueError(part_c)
     vmem = functools.partial(pltpu.VMEM, dtype=jnp.float32)
     scratch = [
         vmem((rows, levels, cols)),
@@ -524,24 +585,28 @@
         vmem((2, part, REACH, LANES)),
         vmem((2, part, REACH, LANES)),
         vmem((2, 2, REACH, REACH, LANES)),
+        *[vmem((part_c, cols_c + 2 * FRONT, LANES))] * 4,
         vmem((wide_c, cols_c + 2 * FRONT, LANES)),
-        vmem((wide_c, cols_c + 2 * FRONT, LANES)),
-        vmem((wide_c, cols_c + 2 * FRONT, LANES)),
+        vmem((wide_long, cols_c + 2 * FRONT, LANES)),
         vmem((wide_c - 2, cols_c + 2 * EDGE, LANES)),
+        vmem((wide_long - 2, cols_c + 2 * EDGE, LANES)),
+        vmem((wide_long - 2, cols_c + 2 * FRONT, LANES)),
+        vmem((wide_c, cols_c + 2 * EDGE, LANES)),
         vmem((part_c, cols_c, LANES)),
         vmem((part_c, cols_c, LANES)),
         vmem((cols_c + 2 * FRONT, LANES)),
         vmem((cols, LANES)),
         vmem((TALLY, LANES)),
-    ] + [pltpu.SemaphoreType.DMA] * 7
-    scratch += [
-        vmem((2, cols_c, LANES)),
-        vmem((2, cols_c + 2 * FRONT, LANES)),
-        vmem((2, COARSE_REACH * part_c, LANES)),
-        vmem((2, COARSE_REACH * part_c, LANES)),
-        vmem((2, 2, COARSE_REACH, LANES)),
-        vmem((2, 2, COARSE_REACH, LANES)),
-    ] * 2
+    ] + [pltpu.SemaphoreType.DMA] * 9
+    for reach in (COARSE_REACH, COARSE_REACH, LONG_REACH, LONG_REACH):
+        scratch += [
+            vmem((2, reach // 2, cols_c, LANES)),
+            vmem((2, reach // 2, cols_c + 2 * FRONT, LANES)),
+            vmem((2, part_c, reach, LANES)),
+            vmem((2, part_c, reach, LANES)),
+            vmem((2, 2, reach // 2, reach, LANES)),
+            vmem((2, 2, reach // 2, reach, LANES)),
+        ]
     in_vmem = pl.BlockSpec(memory_space=pltpu.VMEM)
     handed = pl.pallas_call(
         functools.partial(kernel, sizes, levels, rows, cols),

time: 20 us -> 19.4 us (0.970)
  the two profiles are of different devices: /device:TPU:24 before, /device:TPU:17 now
where the time goes in v6:
time: 19.4 us; the launch traced here: 19.2 us
  Pallas kernels  19.2 us (99%)
    pallas_call x1, Pallas kernels, shards(): pl.pallas_call(functools.partial(kernel, sizes, levels, rows, cols), out_...  18 us
    pallas_call x1, Pallas kernels, shards(): pl.pallas_call(functools.partial(closing, levels, rows), out_shape=jax.Sh...  1.23 us

profile of v6, /device:TPU:17, one launch (start us, length us, event | category | flops | bytes accessed | tf_op | source)
XLA Modules:
  0.0 19.2 jit_solution(15237092699210847528)
XLA Ops:
  0.0 18.0 %parareal.1 = (f32[16,128,128]{2,1,0:T(8,128)S(1)}, f32[6,64,128]{2,1,0:T(8,128)S(1)}) custom-call(f32[64,32,128]{2,1,0:T(8,128)} %bitcast.3, f32[1,64]{1,0:T(1,128)} %bitcast.4, f32[2,64]{1,0:T(2,128)} %wind_hbm.1), custom_call_target="tpu_custom_call" | custom-call | tf_op jit(solution)/shard_map/parareal/pallas_call | solution.py:611
  18.0 1.2 %closing.1 = f32[64,32,128]{2,1,0:T(8,128)} custom-call(f32[16,128,128]{2,1,0:T(8,128)S(1)} %get-tuple-element.7.turned, f32[6,64,128]{2,1,0:T(8,128)S(1)} %get-tuple-element.8.change), custom_call_target="tpu_custom_call" | custom-call | tf_op jit(solution)/shard_map/closing/pallas_call | solution.py:620

commit v7 on v6

--- a/solution.py
+++ b/solution.py
@@ -87,16 +87,14 @@
         pltpu.make_async_copy(source, landing, small_sem).start()
 
     barrier = pltpu.get_barrier_semaphore()
-    odd = tm % 2 == 1
-    partners = [(0, dx, dy) for dx, dy in AROUND] + [(dz, 0, 0) for dz in (-1, 1, -2, 2)]
+    partners = [(0, dx, dy) for dx, dy in AROUND] + [(-1, 0, 0), (1, 0, 0)]
     partners.sort(key=lambda move: -sum(map(abs, move)))
     awaited = jnp.int32(0)
     for move in partners:
         def greet(move=move):
             pl.semaphore_signal(barrier, inc=1, device_id=target(*move), device_id_type=pl.DeviceIdType.MESH)
-        met = jnp.logical_and(odd, there(*move)) if abs(move[0]) == 2 else there(*move)
-        guarded(met, greet)
-        awaited = awaited + met.astype(jnp.int32)
+        guarded(there(*move), greet)
+        awaited = awaited + there(*move).astype(jnp.int32)
 
     def send_all(copies, dz, moves):
         for move in moves:
@@ -169,7 +167,7 @@
     old_strips, new_strips, prior_old_strips, prior_new_strips = (strip_refs[6 * k : 6 * k + 6] for k in range(4))
     old_main = old_own.at[:, pl.ds(FRONT, cols_c)]
     old_copies = coarse_copies(None, old_own, old_strips, old_in, 0)
-    chain_copies = coarse_copies(sent, new_own, new_strips, chain_in, 1)
+    chain_copies = coarse_copies(fine_mean, new_own, new_strips, chain_in, 1)
     prior_old_copies = coarse_copies(old_main, prior_old_own, prior_old_strips, prior_old_in, 1)
     prior_new_copies = coarse_copies(sent, prior_new_own, prior_new_strips, prior_new_in, 2)
     has_next, has_second = tm < n_tm - 1, tm < n_tm - 2
@@ -205,14 +203,14 @@
     high_lanes = lane >= LANES - levels
     pl.semaphore_wait(barrier, awaited)
 
-    @pl.when(tm > 0)
-    def _():
-        pl.semaphore_signal(ready, inc=1, device_id=target(-1, 0, 0), device_id_type=pl.DeviceIdType.MESH)
-
-    @pl.when(jnp.logical_and(odd, tm > 1))
-    def _():
-        pl.semaphore_signal(ready, inc=1, device_id=target(-2, 0, 0), device_id_type=pl.DeviceIdType.MESH)
-
+    def say_ready(k):
+        @pl.when(tm > 0)
+        def _():
+            pl.semaphore_signal(
+                ready.at[k], inc=1, device_id=target(-1, 0, 0), device_id_type=pl.DeviceIdType.MESH
+            )
+
+    say_ready(0)
     pltpu.make_async_copy(small_ref, small_ref, small_sem).wait()
     diffuse = packed(small_ref[0:1, :])
     east_wind = packed(small_ref[1:2, :])
@@ -273,9 +271,6 @@
     def old_row(row, col, count):
         return old_own[row, pl.ds(FRONT + col, count), :]
 
-    def sent_row(row, col, count):
-        return sent[row, pl.ds(col, count), :]
-
     for row in range(part_c):
         old_own[row, pl.ds(FRONT, cols_c), :] = restricted(first, row)
     pack_strips(old_row, old_strips, COARSE_REACH)
@@ -332,21 +327,23 @@
     fill_missing(far_copies, x_moves)
     fill_missing(old_copies, AROUND)
     inner_steps(centre_update)
+
+    @pl.when(has_next)
+    def _():
+        pl.semaphore_wait(ready.at[0], 1)
+        say_ready(1)
+        pack_strips(old_row, prior_old_strips, LONG_REACH)
+        send_all(prior_old_copies, 1, PLANE)
+
+    @pl.when(tm > 0)
+    def _():
+        fill_missing(prior_old_copies, AROUND)
+
     all_arrived(fine_copies, side_in_sem, side_moves)
     for side, (start, mask) in enumerate(reaches):
         for row in range(part):
             first[REACH + row, pl.ds(start, REACH), :] = jnp.where(mask, y_recv[side, row], 0.0)
     inner_steps(sides_update)
-
-    @pl.when(odd)
-    def _():
-        fill_missing(prior_old_copies, AROUND)
-
-    @pl.when(jnp.logical_and(jnp.logical_not(odd), has_next))
-    def _():
-        pl.semaphore_wait(ready, 1)
-        pack_strips(old_row, prior_old_strips, LONG_REACH)
-        send_all(prior_old_copies, 1, PLANE)
 
     def bring_halo(halo_rows):
         for row in halo_rows:
@@ -387,11 +384,9 @@
     for row in range(part_c):
         fine_mean[row] = restricted(fine, row)
 
-    @pl.when(jnp.logical_and(jnp.logical_not(odd), has_next))
-    def _():
-        for row in range(part_c):
-            sent[row] = fine_mean[row]
-        pack_strips(sent_row, new_strips, COARSE_REACH)
+    @pl.when(has_next)
+    def _():
+        pack_strips(lambda row, col, count: fine_mean[row, pl.ds(col, count), :], new_strips, COARSE_REACH)
         send_all(chain_copies, 1, AROUND)
         send_all(chain_copies, 1, ((0, 0),))
 
@@ -455,68 +450,60 @@
     all_arrived(old_copies, old_in, AROUND)
     extend(old_own, old_strips, extended, COARSE_REACH)
     image_of(extended, old_image)
-    pl.when(tm == 0)(lambda: change_of(extended, old_image, COARSE_REACH, change))
+    def send_on():
+        for row in range(part_c):
+            sent[row] = fine_mean[row] + smoothed(change, row, FRONT, cols_c)
+        pack_strips(lambda row, col, count: sent[row, pl.ds(col, count), :], prior_new_strips, LONG_REACH)
+        pl.semaphore_wait(ready.at[1], 1)
+        send_all(prior_new_copies, 2, AROUND)
+        send_all(prior_new_copies, 2, ((0, 0),))
+
+    @pl.when(tm == 0)
+    def _():
+        change_of(extended, old_image, COARSE_REACH, change)
+        pl.when(has_second)(send_on)
 
     @pl.when(tm > 0)
     def _():
         fill_missing(chain_copies, AROUND)
 
-    @pl.when(jnp.logical_and(odd, tm > 1))
+    @pl.when(tm > 1)
     def _():
         fill_missing(prior_new_copies, AROUND)
 
-    @pl.when(odd)
+    for row in range(part):
+        turned[row] = fine[REACH + row, pl.ds(FRONT, cols), :].T
+
+    @pl.when(tm > 0)
     def _():
         all_arrived(prior_old_copies, prior_old_in, PLANE)
         extend(prior_old_own, prior_old_strips, long_extended, LONG_REACH)
         image_of(long_extended, prior_image)
-
-    pl.when(tm == 1)(find_lift)
-
-    for row in range(part):
-        turned[row] = fine[REACH + row, pl.ds(FRONT, cols), :].T
-
-    @pl.when(tm > 0)
-    def _():
+        pl.when(tm == 1)(find_lift)
         all_arrived(chain_copies, chain_in, PLANE)
         extend(new_own, new_strips, extended, COARSE_REACH)
 
-    @pl.when(jnp.logical_and(odd, tm > 1))
-    def _():
-        all_arrived(prior_new_copies, prior_new_in, PLANE)
-        extend(prior_new_own, prior_new_strips, long_extended, LONG_REACH)
-        find_lift()
-
-    @pl.when(odd)
-    def _():
+        @pl.when(tm > 1)
+        def _():
+            all_arrived(prior_new_copies, prior_new_in, PLANE)
+            extend(prior_new_own, prior_new_strips, long_extended, LONG_REACH)
+            find_lift()
+
         for row in range(wide_c):
             extended[row, across, :] = extended[row, across, :] + lift[row]
-
-    pl.when(tm > 0)(lambda: change_of(extended, old_image, COARSE_REACH, change))
-
-    @pl.when(jnp.logical_and(odd, has_next))
-    def _():
-        for row in range(part_c):
-            sent[row] = fine_mean[row] + smoothed(change, row, FRONT, cols_c)
-        pl.semaphore_wait(ready, 1 + has_second.astype(jnp.int32))
-
-        @pl.when(has_second)
-        def _():
-            pack_strips(sent_row, prior_new_strips, LONG_REACH)
-            send_all(prior_new_copies, 2, AROUND)
-            send_all(prior_new_copies, 2, ((0, 0),))
-
-        pack_strips(sent_row, new_strips, COARSE_REACH)
-        send_all(chain_copies, 1, AROUND)
-        send_all(chain_copies, 1, ((0, 0),))
+        change_of(extended, old_image, COARSE_REACH, change)
+        pl.when(has_second)(send_on)
 
     sends_done(fine_copies, 0, y_moves)
     sends_done(old_copies, 0, AROUND)
     sends_done(near_copies, 0, x_moves)
     sends_done(far_copies, 0, x_moves)
-    pl.when(has_next)(lambda: sends_done(chain_copies, 1, PLANE))
-    pl.when(jnp.logical_and(jnp.logical_not(odd), has_next))(lambda: sends_done(prior_old_copies, 1, PLANE))
-    pl.when(jnp.logical_and(odd, has_second))(lambda: sends_done(prior_new_copies, 2, PLANE))
+    @pl.when(has_next)
+    def _():
+        sends_done(chain_copies, 1, PLANE)
+        sends_done(prior_old_copies, 1, PLANE)
+
+    pl.when(has_second)(lambda: sends_done(prior_new_copies, 2, PLANE))
 
 
 def closing(levels, rows, turned, change, out_hbm, filled, spread_rows, sem):
@@ -578,7 +565,7 @@
         vmem((3, levels)),
         pltpu.SemaphoreType.DMA((2,)),
         pltpu.SemaphoreType.DMA,
-        pltpu.SemaphoreType.REGULAR,
+        pltpu.SemaphoreType.REGULAR((2,)),
         vmem((wide, cols + 2 * FRONT, LANES)),
         vmem((wide, cols + 2 * FRONT, LANES)),
         vmem((2, REACH, levels, cols)),

time: 19.4 us -> 18.7 us (0.964)
  the two profiles are of different devices: /device:TPU:17 before, /device:TPU:24 now
where the time goes in v7:
time: 18.7 us; the launch traced here: 18.6 us
  Pallas kernels  18.6 us (99%)
    pallas_call x1, Pallas kernels, shards(): pl.pallas_call(functools.partial(kernel, sizes, levels, rows, cols), out_...  17.3 us
    pallas_call x1, Pallas kernels, shards(): pl.pallas_call(functools.partial(closing, levels, rows), out_shape=jax.Sh...  1.23 us

profile of v7, /device:TPU:24, one launch (start us, length us, event | category | flops | bytes accessed | tf_op | source)
XLA Modules:
  0.0 18.6 jit_solution(1545829268591128602)
XLA Ops:
  0.0 17.3 %parareal.1 = (f32[16,128,128]{2,1,0:T(8,128)S(1)}, f32[6,64,128]{2,1,0:T(8,128)S(1)}) custom-call(f32[64,32,128]{2,1,0:T(8,128)} %bitcast.3, f32[1,64]{1,0:T(1,128)} %bitcast.4, f32[2,64]{1,0:T(2,128)} %wind_hbm.1), custom_call_target="tpu_custom_call" | custom-call | tf_op jit(solution)/shard_map/parareal/pallas_call | solution.py:598
  17.3 1.2 %closing.1 = f32[64,32,128]{2,1,0:T(8,128)} custom-call(f32[16,128,128]{2,1,0:T(8,128)S(1)} %get-tuple-element.7.turned, f32[6,64,128]{2,1,0:T(8,128)S(1)} %get-tuple-element.8.change), custom_call_target="tpu_custom_call" | custom-call | tf_op jit(solution)/shard_map/closing/pallas_call | solution.py:607

commit v8 on v7

--- a/solution.py
+++ b/solution.py
@@ -237,7 +237,6 @@
     bring_own(rows_first)
     send_all(fine_copies, 0, corner_moves)
     send_all(near_copies, 0, x_moves)
-    send_all(far_copies, 0, x_moves)
     load_done(1, rows_later)
     bring_own(rows_later)
     send_all(fine_copies, 0, side_moves)
@@ -274,6 +273,7 @@
     for row in range(part_c):
         old_own[row, pl.ds(FRONT, cols_c), :] = restricted(first, row)
     pack_strips(old_row, old_strips, COARSE_REACH)
+    send_all(far_copies, 0, x_moves)
     send_all(old_copies, 0, AROUND)
 
     def inside_x(row, reach, length):
@@ -333,7 +333,7 @@
         pl.semaphore_wait(ready.at[0], 1)
         say_ready(1)
         pack_strips(old_row, prior_old_strips, LONG_REACH)
-        send_all(prior_old_copies, 1, PLANE)
+        send_all(prior_old_copies, 1, (*side_moves, (0, 0)))
 
     @pl.when(tm > 0)
     def _():
@@ -372,6 +372,7 @@
             pl.loop(0, count)(outer_row)
 
     all_arrived(near_copies, near_in, x_moves)
+    pl.when(has_next)(lambda: send_all(prior_old_copies, 1, x_moves + corner_moves))
     all_arrived(fine_copies, corner_in_sem, corner_moves)
     bring_halo([*range(far, REACH), *range(REACH + part, REACH + part + near)])
     outer_steps(far, 0, near)

time: 18.7 us -> 18.4 us (0.984)
  the two profiles are of different devices: /device:TPU:24 before, /device:TPU:27 now
where the time goes in v8:
time: 18.4 us; the launch traced here: 18.2 us
  Pallas kernels  18.2 us (99%)
    pallas_call x1, Pallas kernels, shards(): pl.pallas_call(functools.partial(kernel, sizes, levels, rows, cols), out_...  17 us
    pallas_call x1, Pallas kernels, shards(): pl.pallas_call(functools.partial(closing, levels, rows), out_shape=jax.Sh...  1.23 us

profile of v8, /device:TPU:27, one launch (start us, length us, event | category | flops | bytes accessed | tf_op | source)
XLA Modules:
  0.0 18.2 jit_solution(6625565976983815253)
XLA Ops:
  0.0 17.0 %parareal.1 = (f32[16,128,128]{2,1,0:T(8,128)S(1)}, f32[6,64,128]{2,1,0:T(8,128)S(1)}) custom-call(f32[64,32,128]{2,1,0:T(8,128)} %bitcast.3, f32[1,64]{1,0:T(1,128)} %bitcast.4, f32[2,64]{1,0:T(2,128)} %wind_hbm.1), custom_call_target="tpu_custom_call" | custom-call | tf_op jit(solution)/shard_map/parareal/pallas_call | solution.py:599
  17.0 1.2 %closing.1 = f32[64,32,128]{2,1,0:T(8,128)} custom-call(f32[16,128,128]{2,1,0:T(8,128)S(1)} %get-tuple-element.7.turned, f32[6,64,128]{2,1,0:T(8,128)S(1)} %get-tuple-element.8.change), custom_call_target="tpu_custom_call" | custom-call | tf_op jit(solution)/shard_map/closing/pallas_call | solution.py:608

commit v9 on v8

--- a/solution.py
+++ b/solution.py
@@ -395,6 +395,8 @@
     begin_c = FRONT - EDGE
     across = pl.ds(begin_c, count_c)
     mask_y = inside_y(begin_c, count_c, cols_c)
+    place_c = lax.broadcasted_iota(jnp.int32, (count_c, LANES), 0) - EDGE
+    mask_near = jnp.logical_and(mask_y, jnp.logical_and(place_c >= -1, place_c <= cols_c))
 
     def extend(buffer, strips, target, reach):
         _, row_in, _, side_in, _, corner_in = strips
@@ -432,7 +434,8 @@
     def change_of(source, image, reach, result):
         for row in range(image.shape[0]):
             moved = advance(source, row + 1, begin_c, count_c, coarse_constants) - image[row]
-            mask = jnp.logical_and(mask_y, inside_x(row + 1, reach, part_c))
+            columns = mask_near if reach == COARSE_REACH else mask_y
+            mask = jnp.logical_and(columns, inside_x(row + 1, reach, part_c))
             result[row, across, :] = jnp.where(mask, moved, 0.0)
 
     def smoothed(source, row, start, count):
@@ -442,11 +445,17 @@
         sides = line[pl.ds(start - 1, count), :] + line[pl.ds(start + 1, count), :]
         return mean_side * sides + mean_mid * line[pl.ds(start, count), :]
 
-    def find_lift():
+    def find_lift(put):
         change_of(long_extended, prior_image, LONG_REACH, prior_change)
         for row in range(wide_c):
             mask = jnp.logical_and(mask_y, inside_x(row, COARSE_REACH, part_c))
-            lift[row] = jnp.where(mask, smoothed(prior_change, row, begin_c, count_c), 0.0)
+            put(row, jnp.where(mask, smoothed(prior_change, row, begin_c, count_c), 0.0))
+
+    def keep_lift(row, value):
+        lift[row] = value
+
+    def add_lift(row, value):
+        extended[row, across, :] = extended[row, across, :] + value
 
     all_arrived(old_copies, old_in, AROUND)
     extend(old_own, old_strips, extended, COARSE_REACH)
@@ -480,7 +489,7 @@
         all_arrived(prior_old_copies, prior_old_in, PLANE)
         extend(prior_old_own, prior_old_strips, long_extended, LONG_REACH)
         image_of(long_extended, prior_image)
-        pl.when(tm == 1)(find_lift)
+        pl.when(tm == 1)(lambda: find_lift(keep_lift))
         all_arrived(chain_copies, chain_in, PLANE)
         extend(new_own, new_strips, extended, COARSE_REACH)
 
@@ -488,10 +497,13 @@
         def _():
             all_arrived(prior_new_copies, prior_new_in, PLANE)
             extend(prior_new_own, prior_new_strips, long_extended, LONG_REACH)
-            find_lift()
-
-        for row in range(wide_c):
-            extended[row, across, :] = extended[row, across, :] + lift[row]
+            find_lift(add_lift)
+
+        @pl.when(tm == 1)
+        def _():
+            for row in range(wide_c):
+                add_lift(row, lift[row])
+
         change_of(extended, old_image, COARSE_REACH, change)
         pl.when(has_second)(send_on)
 
@@ -521,15 +533,15 @@
         for distance, weights in ((-1, weights_low), (0, weights_mid), (1, weights_high)):
             chosen = jnp.logical_and(offset_of == o, apart == distance)
             spreading = jnp.where(chosen, weights[o], spreading)
-    spreading = jnp.concatenate([spreading.astype(jnp.bfloat16)] * 3, axis=0)
+    spreading = spreading.astype(jnp.bfloat16)
+
     def spread_row(row):
-        rest, pieces = change[row, pl.ds(FRONT - EDGE, count_c), :], []
+        rest, total = change[row, pl.ds(FRONT - EDGE, count_c), :].T, 0.0
         for _ in range(3):
-            piece = rest.astype(jnp.bfloat16).astype(jnp.float32)
-            pieces.append(piece)
-            rest = rest - piece
-        split = jnp.concatenate(pieces, axis=0).T.astype(jnp.bfloat16)
-        return jnp.dot(split, spreading, preferred_element_type=jnp.float32)
+            piece = rest.astype(jnp.bfloat16)
+            total = total + jnp.dot(piece, spreading, preferred_element_type=jnp.float32)
+            rest = rest - piece.astype(jnp.float32)
+        return total
 
     for row in range(2):
         spread_rows[row] = spread_row(row)

time: 18.4 us -> 18.4 us (level)
  no operation moved by 1% of the time
where the time goes in v9:
time: 18.4 us; the launch traced here: 18.2 us
  Pallas kernels  18.2 us (99%)
    pallas_call x1, Pallas kernels, shards(): pl.pallas_call(functools.partial(kernel, sizes, levels, rows, cols), out_...  16.9 us
    pallas_call x1, Pallas kernels, shards(): pl.pallas_call(functools.partial(closing, levels, rows), out_shape=jax.Sh...  1.29 us

profile of v9, /device:TPU:27, one launch (start us, length us, event | category | flops | bytes accessed | tf_op | source)
XLA Modules:
  0.0 18.2 jit_solution(1457854618208921544)
XLA Ops:
  0.0 16.9 %parareal.1 = (f32[16,128,128]{2,1,0:T(8,128)S(1)}, f32[6,64,128]{2,1,0:T(8,128)S(1)}) custom-call(f32[64,32,128]{2,1,0:T(8,128)} %bitcast.3, f32[1,64]{1,0:T(1,128)} %bitcast.4, f32[2,64]{1,0:T(2,128)} %wind_hbm.1), custom_call_target="tpu_custom_call" | custom-call | tf_op jit(solution)/shard_map/parareal/pallas_call | solution.py:611
  17.0 1.3 %closing.1 = f32[64,32,128]{2,1,0:T(8,128)} custom-call(f32[16,128,128]{2,1,0:T(8,128)S(1)} %get-tuple-element.7.turned, f32[6,64,128]{2,1,0:T(8,128)S(1)} %get-tuple-element.8.change), custom_call_target="tpu_custom_call" | custom-call | tf_op jit(solution)/shard_map/closing/pallas_call | solution.py:620

commit v10 on v9

--- a/solution.py
+++ b/solution.py
@@ -533,15 +533,16 @@
         for distance, weights in ((-1, weights_low), (0, weights_mid), (1, weights_high)):
             chosen = jnp.logical_and(offset_of == o, apart == distance)
             spreading = jnp.where(chosen, weights[o], spreading)
-    spreading = spreading.astype(jnp.bfloat16)
+    spreading = jnp.concatenate([spreading.astype(jnp.bfloat16)] * 3, axis=0)
 
     def spread_row(row):
-        rest, total = change[row, pl.ds(FRONT - EDGE, count_c), :].T, 0.0
+        rest, pieces = change[row, pl.ds(FRONT - EDGE, count_c), :], []
         for _ in range(3):
-            piece = rest.astype(jnp.bfloat16)
-            total = total + jnp.dot(piece, spreading, preferred_element_type=jnp.float32)
-            rest = rest - piece.astype(jnp.float32)
-        return total
+            piece = rest.astype(jnp.bfloat16).astype(jnp.float32)
+            pieces.append(piece)
+            rest = rest - piece
+        split = jnp.concatenate(pieces, axis=0).T.astype(jnp.bfloat16)
+        return jnp.dot(split, spreading, preferred_element_type=jnp.float32)
 
     for row in range(2):
         spread_rows[row] = spread_row(row)

time: 18.4 us -> 18.4 us (level)
  no operation moved by 1% of the time
where the time goes in v10:
time: 18.4 us; the launch traced here: 18.2 us
  Pallas kernels  18.2 us (99%)
    pallas_call x1, Pallas kernels, shards(): pl.pallas_call(functools.partial(kernel, sizes, levels, rows, cols), out_...  16.9 us
    pallas_call x1, Pallas kernels, shards(): pl.pallas_call(functools.partial(closing, levels, rows), out_shape=jax.Sh...  1.23 us

profile of v10, /device:TPU:27, one launch (start us, length us, event | category | flops | bytes accessed | tf_op | source)
XLA Modules:
  0.0 18.2 jit_solution(11474364255485495657)
XLA Ops:
  0.0 16.9 %parareal.1 = (f32[16,128,128]{2,1,0:T(8,128)S(1)}, f32[6,64,128]{2,1,0:T(8,128)S(1)}) custom-call(f32[64,32,128]{2,1,0:T(8,128)} %bitcast.3, f32[1,64]{1,0:T(1,128)} %bitcast.4, f32[2,64]{1,0:T(2,128)} %wind_hbm.1), custom_call_target="tpu_custom_call" | custom-call | tf_op jit(solution)/shard_map/parareal/pallas_call | solution.py:612
  17.0 1.2 %closing.1 = f32[64,32,128]{2,1,0:T(8,128)} custom-call(f32[16,128,128]{2,1,0:T(8,128)S(1)} %get-tuple-element.7.turned, f32[6,64,128]{2,1,0:T(8,128)S(1)} %get-tuple-element.8.change), custom_call_target="tpu_custom_call" | custom-call | tf_op jit(solution)/shard_map/closing/pallas_call | solution.py:621

commit v11 on v10

--- a/solution.py
+++ b/solution.py
@@ -471,7 +471,6 @@
     @pl.when(tm == 0)
     def _():
         change_of(extended, old_image, COARSE_REACH, change)
-        pl.when(has_second)(send_on)
 
     @pl.when(tm > 0)
     def _():
@@ -483,6 +482,8 @@
 
     for row in range(part):
         turned[row] = fine[REACH + row, pl.ds(FRONT, cols), :].T
+
+    pl.when(jnp.logical_and(tm == 0, has_second))(send_on)
 
     @pl.when(tm > 0)
     def _():

time: 18.4 us -> 18.4 us (level)
  no operation moved by 1% of the time
where the time goes in v11:
time: 18.4 us; the launch traced here: 18.2 us
  Pallas kernels  18.2 us (99%)
    pallas_call x1, Pallas kernels, shards(): pl.pallas_call(functools.partial(kernel, sizes, levels, rows, cols), out_...  17 us
    pallas_call x1, Pallas kernels, shards(): pl.pallas_call(functools.partial(closing, levels, rows), out_shape=jax.Sh...  1.23 us

profile of v11, /device:TPU:27, one launch (start us, length us, event | category | flops | bytes accessed | tf_op | source)
XLA Modules:
  0.0 18.2 jit_solution(10439027100192030118)
XLA Ops:
  0.0 17.0 %parareal.1 = (f32[16,128,128]{2,1,0:T(8,128)S(1)}, f32[6,64,128]{2,1,0:T(8,128)S(1)}) custom-call(f32[64,32,128]{2,1,0:T(8,128)} %bitcast.3, f32[1,64]{1,0:T(1,128)} %bitcast.4, f32[2,64]{1,0:T(2,128)} %wind_hbm.1), custom_call_target="tpu_custom_call" | custom-call | tf_op jit(solution)/shard_map/parareal/pallas_call | solution.py:613
  17.0 1.2 %closing.1 = f32[64,32,128]{2,1,0:T(8,128)} custom-call(f32[16,128,128]{2,1,0:T(8,128)S(1)} %get-tuple-element.7.turned, f32[6,64,128]{2,1,0:T(8,128)S(1)} %get-tuple-element.8.change), custom_call_target="tpu_custom_call" | custom-call | tf_op jit(solution)/shard_map/closing/pallas_call | solution.py:622
